TPU v7x, 128 devices: a whole 4x4x4 slice. The times are simulated.
128 devices in a mesh: row: 8 (over y, core), col: 16 (over z, x).
Axes of the slice: x: 4, y: 4, z: 4, core: 2. Of those that a mesh axis runs over, the one named last changes fastest.
Arguments:
- features: float32 [256, 1024, 128], P('row', 'col'), may hold values from -0.4 to 0.4
- step_size: float32 [256, 1024, 128], P('row', 'col'), may hold values from 0.5 to 2
- write_weights: float32 [256, 1024, 16], P('row', 'col'), may hold values from -6 to 6
- read_weights: float32 [256, 1024, 16], P('row', 'col'), may hold values from -6 to 6
- decay_log: float32 [16, 128], replicated, may hold values from -7.6 to -3.5
- out_grad: float32 [256, 1024, 128], P('row', 'col'), may hold values from -0.4 to 0.4
Outputs:
- grad_features: float32 [256, 1024, 128], P('row', 'col')
- grad_step: float32 [256, 1024, 128], P('row', 'col')
- grad_write: float32 [256, 1024, 16], P('row', 'col')
- grad_read: float32 [256, 1024, 16], P('row', 'col')
- grad_decay: float32 [16, 128], replicated
All inputs are finite; a program needn't handle non-finite values.
Results may differ from a plain program's by a relative error of at most 0.0002.
Values sent between devices are 32-bit elements; how exact they have to be, the bound alone decides.
A program may use at most 320 MiB of HBM per device.

v0:
```python
import jax
import jax.numpy as jnp
from jax import lax
from jax.sharding import PartitionSpec as P


def carried_in(shard, axis, combine, identity, reverse):
    size, mine = (lax.axis_size(axis), lax.axis_index(axis))
    everything = jax.tree.map(lambda part: lax.all_gather(part, axis), shard)
    start = jax.tree.map(
        lambda part, zero: jnp.broadcast_to(jnp.asarray(zero, part.dtype), part.shape),
        shard,
        identity,
    )

    def lap(k, before):
        at = size - 1 - k if reverse else k
        reached = at > mine if reverse else at < mine
        new = combine(before, jax.tree.map(lambda part: part[at], everything))
        return jax.tree.map(lambda a, b: jnp.where(reached, a, b), new, before)

    return lax.fori_loop(0, size, lap, start)


def sweep_rows(decays, driving, backward):

    def advance(current, inputs):
        factor, source = inputs
        current = factor * current + source
        return (current, current)

    def retreat(passed, inputs):
        factor, source = inputs
        adjoint = source + passed
        return (factor * adjoint, adjoint)

    initial = jnp.zeros(decays.shape[1:], jnp.float32)
    if backward:
        closing, values = lax.scan(retreat, initial, (decays, driving), reverse=True)
    else:
        closing, values = lax.scan(advance, initial, (decays, driving))
    return (values, closing)


def sweep_cols(decays, driving, backward):
    length = decays.shape[1]

    def advance(index, running):
        current, values = running
        place = length - 1 - index if backward else index
        place = jnp.asarray(place).astype(jnp.int32)
        factor = lax.dynamic_index_in_dim(decays, place, 1, keepdims=False)
        source = lax.dynamic_index_in_dim(driving, place, 1, keepdims=False)
        if backward:
            value = source + current
            values = lax.dynamic_update_index_in_dim(values, value, place, 1)
            current = factor * value
        else:
            current = factor * current + source
            values = lax.dynamic_update_index_in_dim(values, current, place, 1)
        return (current, values)

    initial = jnp.zeros(decays.shape[:1] + decays.shape[2:], jnp.float32)
    closing, values = lax.fori_loop(0, length, advance, (initial, jnp.zeros_like(driving)))
    return (values, closing)


def link_parts(final_state, exponent_sum, decay_rate):

    def combine(earlier, subsequent):
        return (earlier[0] * subsequent[0], subsequent[0] * earlier[1] + subsequent[1])

    products = jnp.exp(exponent_sum[:, None, :] * decay_rate)
    element = (products, final_state)
    identity = (jnp.ones_like(products), jnp.zeros_like(final_state))
    return (element, identity, combine)


def shards(features, step_size, write_weights, read_weights, decay_log, out_grad):
    highest = lax.Precision.HIGHEST
    decay_rate = -jnp.exp(decay_log)
    decays = jnp.exp(step_size[:, :, None, :] * decay_rate)
    driving = step_size[:, :, None, :] * write_weights[:, :, :, None] * features[:, :, None, :]
    running_rows = jnp.cumsum(step_size, 0)
    running_cols = jnp.cumsum(step_size, 1)
    sum_rows = running_rows[-1]
    sum_cols = running_cols[:, -1]
    local_rows, leaving_rows = sweep_rows(decays, driving, False)
    element, identity, combine = link_parts(leaving_rows, sum_rows, decay_rate)
    from_above = carried_in(element, "row", combine, identity, False)[1]
    vertical = local_rows + jnp.exp(running_rows[:, :, None, :] * decay_rate) * from_above[None]
    vert_prev = jnp.concatenate([from_above[None], vertical[:-1]], 0)
    local_cols, leaving_cols = sweep_cols(decays, vertical, False)
    element, identity, combine = link_parts(leaving_cols, sum_cols, decay_rate)
    from_left = carried_in(element, "col", combine, identity, False)[1]
    states = local_cols + jnp.exp(running_cols[:, :, None, :] * decay_rate) * from_left[:, None]
    states_prev = jnp.concatenate([from_left[:, None], states[:, :-1]], 1)
    direct = read_weights[:, :, :, None] * out_grad[:, :, None, :]
    adjoint_local, outgoing_cols = sweep_cols(decays, direct, True)
    element, identity, combine = link_parts(outgoing_cols, sum_cols, decay_rate)
    from_right = carried_in(element, "col", combine, identity, True)[1]
    after_cols = sum_cols[:, None, :] - running_cols
    adjoint_h = (
        adjoint_local + jnp.exp(after_cols[:, :, None, :] * decay_rate) * from_right[:, None]
    )
    adjoint_vlocal, outgoing_rows = sweep_rows(decays, adjoint_h, True)
    element, identity, combine = link_parts(outgoing_rows, sum_rows, decay_rate)
    from_below = carried_in(element, "row", combine, identity, True)[1]
    after_rows = sum_rows[None] - running_rows
    adjoint_v = adjoint_vlocal + jnp.exp(after_rows[:, :, None, :] * decay_rate) * from_below[None]
    exponent_grad = (adjoint_h * states_prev + adjoint_v * vert_prev) * decays
    through = jnp.einsum("hwnd,hwn->hwd", adjoint_v, write_weights, precision=highest)
    grad_features = step_size * through
    grad_step = features * through + jnp.einsum(
        "hwnd,nd->hwd", exponent_grad, decay_rate, precision=highest
    )
    grad_write = jnp.einsum("hwnd,hwd->hwn", adjoint_v, step_size * features, precision=highest)
    grad_read = jnp.einsum("hwnd,hwd->hwn", states, out_grad, precision=highest)
    partial_sum = jnp.einsum("hwnd,hwd->nd", exponent_grad, step_size, precision=highest)
    grad_decay = lax.psum(partial_sum, ("row", "col")) * decay_rate
    return (grad_features, grad_step, grad_write, grad_read, grad_decay)


def solution(mesh):
    in_specs = (
        P("row", "col", None),
        P("row", "col", None),
        P("row", "col", None),
        P("row", "col", None),
        P(),
        P("row", "col", None),
    )
    out_specs = (
        P("row", "col", None),
        P("row", "col", None),
        P("row", "col", None),
        P("row", "col", None),
        P(),
    )
    return jax.shard_map(shards, mesh=mesh, in_specs=in_specs, out_specs=out_specs, check_vma=False)
```

profile of v0, /device:TPU:1, one launch (start us, length us, event | category | flops | bytes accessed | tf_op | source)
XLA Modules:
  0.0 968.1 jit_solution(15481916507911445551)
XLA Ops:
  13.7 9.3 multiply_multiply_fusion
  23.0 5.8 copy-done
  28.8 6.2 copy.32
  35.0 7.9 broadcast.59.clone3
  42.9 79.4 %while.128 = (s32[]{:T(128)}, f32[64,16,128]{2,1,0:T(8,128)S(1)}, f32[32,64,16,128]{3,2,0,1:T(8,128)}, f32[32,64,16,128]{3,2,1,0:T(8,128)}, f32[32,64,16,128]{3,2,0,1:T(8,128)}, /*index=5*/s32[]{:T(128)}, s32[]{:T(128)}) while((s32[]{:T(128)}, f32[64,16,128]{2,1,0:T(8,128)S(1)}, f32[32,64,16,128]{3,2,0,1:T(8,128)}, ...), condition=%wide.region_11.12_spmd.clone, body=%wide.region_10.11_spmd.clone.sunk | while | flops 393219 | bytes 2622039 | solution.py:41
  42.9 2.5 bitcast_dynamic-update-slice_fusion.10
  45.4 2.5 bitcast_dynamic-update-slice_fusion.10
  47.9 2.5 bitcast_dynamic-update-slice_fusion.10
  50.4 2.5 bitcast_dynamic-update-slice_fusion.10
  52.9 2.5 bitcast_dynamic-update-slice_fusion.10
  57.9 2.5 bitcast_dynamic-update-slice_fusion.10
  60.4 2.5 bitcast_dynamic-update-slice_fusion.10
  62.8 2.5 bitcast_dynamic-update-slice_fusion.10
  65.3 2.5 bitcast_dynamic-update-slice_fusion.10
  67.8 2.5 bitcast_dynamic-update-slice_fusion.10
  70.3 2.5 bitcast_dynamic-update-slice_fusion.10
  82.6 2.5 bitcast_dynamic-update-slice_fusion.10
  90.1 2.5 bitcast_dynamic-update-slice_fusion.10
  95.0 2.5 bitcast_dynamic-update-slice_fusion.10
  97.5 2.5 bitcast_dynamic-update-slice_fusion.10
  109.9 2.5 bitcast_dynamic-update-slice_fusion.10
  119.8 2.5 bitcast_dynamic-update-slice_fusion.10
  123.2 4.0 fusion.18
  134.2 7.6 broadcast_multiply_fusion
  141.8 8.0 broadcast.59.clone3.2
  149.7 186.2 %while.124 = (s32[]{:T(128)}, f32[32,16,128]{2,1,0:T(8,128)S(1)}, f32[32,64,16,128]{3,2,0,1:T(8,128)}, f32[32,64,16,128]{3,2,0,1:T(8,128)}, f32[32,64,16,128]{3,...) while((s32[]{:T(128)}, f32[32,16,128]{2,1,0:T(8,128)S(1)}, ...), condition=%wide.region_1.2_spmd.clone, body=%wide.region_0.0_spmd.clone.sunk | while | flops 327687 | bytes 1835166 | solution.py:64
  338.5 13.5 %while.129 = (s32[]{:T(128)}, f32[64,16,128]{2,1,0:T(8,128)S(1)}, s32[]{:T(128)}, f32[8,64,16,128]{3,2,1,0:T(8,128)}, f32[8,64,16,128]{3,2,1,0:T(8,128)}, /*index=5*/s32[]{:T(128)}, s32[]{:T(128)}) while((s32[]{:T(128)}, f32[64,16,128]{2,1,0:T(8,128)S(1)}, s32[]{:T(128)}, f32[8,64,16,128]{3,2,1,0:T(8,128)}, ...), condition=%wide.region_13.14_spmd.clone, body=%wide.region_12.13_spmd.clone.sunk | while | flops 524292 | bytes 2097253 | solution.py:22
  352.0 12.2 %multiply_add_fusion.1 = f32[32,64,16,128]{3,2,0,1:T(8,128)} fusion(f32[32,64,16,128]{3,2,0,1:T(8,128)} %get-tuple-element.823, f32[64,16,128]{2,1,0:T(8,128)S(1)} %get-tuple-element.825, f32[32,64,128]{2,0,1:T(8,128)} %copy.41, f32[16,128]{1,0:T(8,128)S(1)} %exponential_negate_fusion), kind=kLoop, calls=%fused_computation.33 | loop fusion | flops 12582912 | bytes 35135488 | tf_op jit(solution)/shard_map/add | solution.py:91
  364.2 8.0 broadcast.59.clone3.1
  372.2 124.9 %while.130 = (s32[]{:T(128)}, f32[32,16,128]{2,1,0:T(8,128)S(1)}, f32[32,64,16,128]{3,2,0,1:T(8,128)}, f32[32,64,16,128]{3,2,0,1:T(8,128)}, f32[32,64,16,128]{3,2,0,1:T(8,128)}, /*index=5*/s32[]{:T(128)}, s32[]{:T(128)}) while((s32[]{:T(128)}, f32[32,16,128]{2,1,0:T(8,128)S(1)}, f32[32,64,16,128]{3,2,0,1:T(8,128)}, ...), condition=%wide.region_15.16_spmd.clone, body=%wide.region_14.15_spmd.clone.sunk | while | flops 196611 | bytes 1311319 | solution.py:64
  500.2 29.8 %while.125 = (s32[]{:T(128)}, f32[32,16,128]{2,1,0:T(8,128)}, s32[]{:T(128)}, f32[16,32,16,128]{3,2,1,0:T(8,128)}, f32[16,32,16,128]{3,2,1,0:T(8,128)}, /*index=5*/s32[]{:T(128)}, s32[]{:T(128)}, s32[]{:T(128)}, s32[]{:T(128)}) while((s32[]{:T(128)}, f32[32,16,128]{2,1,0:T(8,128)}, s32[]{:T(128)}, f32[16,32,16,128]{3,2,1,0:T(8,128)}, ...), condition=%wide.region_4.5_spmd.clone, body=%wide.region_3.4_spmd.clone.sunk | while | flops 262152 | bytes 1048739 | solution.py:22
  530.0 22.9 %all-gather.21.cloned.1.call-done = f32[512,16,128]{2,1,0:T(8,128)} async-done(((f32[32,16,128]{2,1,0:T(8,128)}), f32[512,16,128]{2,1,0:T(8,128)}) %all-gather.21.cloned.1.call-update) | async-done | bytes 4194320 | tf_op jit(solution)/shard_map/all_gather | solution.py:9
  552.9 20.3 %while.131 = (s32[]{:T(128)}, f32[32,16,128]{2,1,0:T(8,128)S(1)}, s32[]{:T(128)}, f32[16,32,16,128]{3,2,1,0:T(8,128)}, f32[16,32,16,128]{3,2,1,0:T(8,128)}, /*index=5*/s32[]{:T(128)}, s32[]{:T(128)}) while((s32[]{:T(128)}, f32[32,16,128]{2,1,0:T(8,128)S(1)}, s32[]{:T(128)}, f32[16,32,16,128]{3,2,1,0:T(8,128)}, ...), condition=%wide.region_17.18_spmd.clone, body=%wide.region_16.17_spmd.clone.sunk | while | flops 262148 | bytes 1048677 | solution.py:22
  573.2 23.2 %multiply_add_fusion = (f32[32,64,16,128]{3,2,0,1:T(8,128)}, f32[32,64,16,128]{3,2,0,1:T(8,128)}) fusion(f32[32,64,16,128]{3,2,0,1:T(8,128)} %get-tuple-element.828, f32[32,16,128]{2,1,0:T(8,128)S(1)} %get-tuple-element.827, f32[32,64,128]{2,0,1:T(8,128)} %copy-done.5, f32[16,128]{1,0:T(8,128)S(1)} %exponential_negate_fusion, ...), kind=kLoop, calls=%fused_computation.32 | loop fusion | flops 25165824 | bytes 69738496 | tf_op jit(solution)/shard_map/add | solution.py:96
  596.4 7.9 broadcast.59.clone2
  604.3 113.4 %while.126 = (s32[]{:T(128)}, f32[64,16,128]{2,1,0:T(8,128)S(1)}, f32[32,64,16,128]{3,2,0,1:T(8,128)}, f32[32,64,16,128]{3,2,1,0:T(8,128)}, f32[32,64,16,128]{3,...) while((s32[]{:T(128)}, f32[64,16,128]{2,1,0:T(8,128)S(1)}, f32[32,64,16,128]{3,2,0,1:T(8,128)}, ...), condition=%wide.region_6.7_spmd.clone, body=%wide.region_5.6_spmd.clone.sunk | while | flops 655364 | bytes 3670132 | solution.py:39
  721.8 2.9 copy.44
  724.7 11.6 %slice.19 = f32[31,64,16,128]{3,2,0,1:T(8,128)} slice(f32[32,64,16,128]{3,2,0,1:T(8,128)} %get-tuple-element.1542), slice={[0:31], [0:64], [0:16], [0:128]} | slice | bytes 32505856 | tf_op jit(solution)/shard_map/slice | solution.py:92
  736.3 13.9 %slice.18 = f32[32,63,16,128]{3,2,0,1:T(8,128)} slice(f32[32,64,16,128]{3,2,0,1:T(8,128)} %get-tuple-element.1087), slice={[0:32], [0:63], [0:16], [0:128]} | slice | bytes 33030144 | tf_op jit(solution)/shard_map/slice | solution.py:97
  753.5 27.6 %fusion.6 = f32[32,64,1,16]{3,2,1,0:T(1,128)} fusion(f32[32,64,128,1]{2,3,1,0:T(1,128)S(1)} %bitcast.158, f32[32,64,16,128]{3,2,0,1:T(8,128)S(1)} %bitcast.152), kind=kOutput, calls=%fused_computation.29 | convolution fusion | flops 50331648 | bytes 17956864 | tf_op jit(solution)/shard_map/hwnd,hwd->hwn/dot_general | solution.py:118
  781.1 2.9 copy.57
  784.1 13.5 %while.127 = (s32[]{:T(128)}, f32[64,16,128]{2,1,0:T(8,128)S(1)}, s32[]{:T(128)}, f32[8,64,16,128]{3,2,1,0:T(8,128)}, f32[8,64,16,128]{3,2,1,0:T(8,128)}, /*index=5*/s32[]{:T(128)}, s32[]{:T(128)}, s32[]{:T(128)}, s32[]{:T(128)}) while((s32[]{:T(128)}, f32[64,16,128]{2,1,0:T(8,128)S(1)}, s32[]{:T(128)}, ...), condition=%wide.region_9.10_spmd.clone, body=%wide.region_8.9_spmd.clone.sunk | while | flops 524296 | bytes 2097315 | solution.py:22
  797.6 34.8 %multiply_reduce_fusion = (f32[128,16]{0,1:T(8,128)S(1)}, f32[32,64,16,128]{3,2,0,1:T(8,128)}, f32[32,64,16,128]{3,2,0,1:T(8,128)}) fusion(f32[128,32,64]{0,1,2:T(8,128)} %copy.74, f32[16,128]{1,0:T(8,128)S(1)} %exponential_negate_fusion, f32[32,64,128]{2,0,1:T(8,128)S(1)} %copy-done.7, f32[31,64,16,128]{3,2,0,1:T(8,128)} %slice.19, ...), kind=kLoop, calls=%fused_computation.28 | loop fusion | flops 50329600 | bytes 104349696 | tf_op jit(solution)/shard_map/hwnd,hwd->nd/dot_general | solution.py:119
  832.3 64.6 %psum.7 = f32[16,128]{1,0:T(8,128)S(1)} all-reduce(f32[16,128]{1,0:T(8,128)S(1)} %bitcast.166), channel_id=1, replica_groups=mesh['row'=8,'col'=16] {'row','col'}, use_global_device_ids=true, to_apply=%region_18.19 | all-reduce | flops 2048 | bytes 16384 | tf_op jit(solution)/shard_map/psum | solution.py:120
  897.5 18.2 %fusion.10 = f32[32,64,1,128]{3,2,1,0:T(1,128)S(1)} fusion(f32[32,64,16,1]{2,3,1,0:T(1,128)} %copy.44, f32[32,64,16,128]{3,2,0,1:T(8,128)} %get-tuple-element.1079), kind=kOutput, calls=%fused_computation.40 | convolution fusion | flops 50331648 | bytes 17956864 | tf_op jit(solution)/shard_map/hwnd,hwn->hwd/dot_general | solution.py:112
  915.7 10.9 %multiply_reduce_fusion.1 = f32[128,32,64]{0,1,2:T(8,128)} fusion(f32[32,64,16,128]{3,2,0,1:T(8,128)} %get-tuple-element.1078, f32[128,16]{0,1:T(8,128)S(1)} %get-tuple-element.1086), kind=kLoop, calls=%fused_computation.31 | loop fusion | flops 8126464 | bytes 17833984
  926.6 3.6 fusion.17
  930.2 28.9 %fusion.8 = f32[32,64,1,16]{3,2,1,0:T(1,128)S(1)} fusion(f32[32,64,128,1]{2,3,1,0:T(1,128)S(1)} %bitcast.157, f32[32,64,16,128]{3,2,0,1:T(8,128)} %get-tuple-element.1079), kind=kOutput, calls=%fused_computation.38 | convolution fusion | flops 50331648 | bytes 17956864 | tf_op jit(solution)/shard_map/hwnd,hwd->hwn/dot_general | solution.py:117
  (394 shorter events, 565.5 us)
Async XLA Ops:
  7.2 331.3 %all-gather.19.cloned.1.call-start = ((), (), s32[]{:S(2)}) async-start(), calls=%async_computation.4 | async-start | bytes 4718592 | tf_op jit(solution)/shard_map/all_gather | solution.py:9
  9.8 13.2 %copy-start.6 = (f32[32,64,128]{2,0,1:T(8,128)}, f32[32,64,128]{2,0,1:T(8,128)S(1)}, u32[]{:S(2)}) copy-start(f32[32,64,128]{2,0,1:T(8,128)S(1)} %copy.27) | copy-start | bytes 3145732
  23.0 5.8 copy-start
  35.0 88.2 %copy-start.3 = (f32[32,64,128]{2,1,0:T(8,128)S(1)}, f32[32,64,128]{2,1,0:T(8,128)}, u32[]{:S(2)}) copy-start(f32[32,64,128]{2,1,0:T(8,128)} %param.23) | copy-start | bytes 3145732
  35.0 95.6 %copy-start.10 = (f32[32,64,16]{1,2,0:T(8,128)S(1)}, f32[32,64,16]{1,2,0:T(8,128)}, u32[]{:S(2)}) copy-start(f32[32,64,16]{1,2,0:T(8,128)} %param.25) | copy-start | bytes 393220
  122.3 0.8 copy-start.4
  123.1 215.4 %all-gather.13.cloned.1.call-start = ((), (), s32[]{:S(2)}) async-start(), calls=%async_computation.1 | async-start | bytes 4718592 | tf_op jit(solution)/shard_map/all_gather | solution.py:9
  128.1 372.1 %all-gather.11.cloned.1.call-start = ((), (), s32[]{:S(2)}) async-start(), calls=%async_computation | async-start | bytes 4456448 | tf_op jit(solution)/shard_map/all_gather | solution.py:9
  128.7 1.0 copy-start.5
  130.5 369.7 %all-gather.15.cloned.1.call-start = ((), (), s32[]{:S(2)}) async-start(), calls=%async_computation.2 | async-start | bytes 4456448 | tf_op jit(solution)/shard_map/all_gather | solution.py:9
  336.0 0.7 copy-start.2
  336.7 216.2 %all-gather.21.cloned.1.call-start = ((), (), s32[]{:S(2)}) async-start(), calls=%async_computation.5 | async-start | bytes 4456448 | tf_op jit(solution)/shard_map/all_gather | solution.py:9
  497.1 0.7 copy-start.8
  497.8 286.3 %all-gather.17.cloned.1.call-start = ((), (), s32[]{:S(2)}) async-start(), calls=%async_computation.3 | async-start | bytes 4718592 | tf_op jit(solution)/shard_map/all_gather | solution.py:9
  717.7 0.8 copy-start.1
  736.2 14.0 %slice-start = ((s8[16777216]{0:T(1024)(128)(4,1)}), s8[4194304]{0:T(1024)(128)(4,1)S(1)}, s32[]{:S(2)}) async-start(s8[16777216]{0:T(1024)(128)(4,1)} %bitcast.151), calls=%async_computation.6 | async-start | bytes 8388608
  736.2 14.0 %copy-start.9 = (f32[32,64,128]{2,1,0:T(8,128)S(1)}, f32[32,64,128]{2,1,0:T(8,128)}, u32[]{:S(2)}) copy-start(f32[32,64,128]{2,1,0:T(8,128)} %param.27) | copy-start | bytes 3145732
  736.2 14.6 %slice-start.1 = ((s8[16777216]{0:T(1024)(128)(4,1)}), s8[4194304]{0:T(1024)(128)(4,1)S(1)}, s32[]{:S(2)}) async-start(s8[16777216]{0:T(1024)(128)(4,1)} %bitcast.151), calls=%async_computation.7 | async-start | bytes 8388608
  736.3 16.1 %slice-start.2 = ((s8[16777216]{0:T(1024)(128)(4,1)}), s8[4194304]{0:T(1024)(128)(4,1)S(1)}, s32[]{:S(2)}) async-start(s8[16777216]{0:T(1024)(128)(4,1)} %bitcast.151), calls=%async_computation.8 | async-start | bytes 8388608
  736.3 17.2 %slice-start.3 = ((s8[16777216]{0:T(1024)(128)(4,1)}), s8[4194304]{0:T(1024)(128)(4,1)S(1)}, s32[]{:S(2)}) async-start(s8[16777216]{0:T(1024)(128)(4,1)} %bitcast.151), calls=%async_computation.9 | async-start | bytes 8388608
  753.5 44.0 %copy-start.7 = (f32[32,64,128]{2,0,1:T(8,128)S(1)}, f32[32,64,128]{2,0,1:T(8,128)}, u32[]{:S(2)}) copy-start(f32[32,64,128]{2,0,1:T(8,128)} %copy-done.6) | copy-start | bytes 3145732
  797.6 99.3 %copy-start.11 = (f32[16,128]{1,0:T(8,128)S(1)}, f32[16,128]{1,0:T(8,128)}, u32[]{:S(2)}) copy-start(f32[16,128]{1,0:T(8,128)} %param.26) | copy-start | bytes 24580
Sparse Core Ops, SparseCore 0:
  123.2 35.7 all-gather.18
  160.7 32.0 all-gather.12
  195.6 51.1 all-gather.10
  336.8 54.8 all-gather.14
  497.9 54.8 all-gather.20
  718.6 32.1 all-gather.16
where the time goes:
time: 984 us; the launch traced here: 968 us
  other arithmetic  690 us (70%)
  local copies, waits for them, and re-layouts  98.4 us (10%)
  matrix products  74.7 us (8%)
  blocking collectives  64.6 us (7%)
  waiting for transfers between devices  23 us (2%)
  between operations  14.6 us (1%)
    dynamic_update_slice x64, other arithmetic, sweep_rows(): closing, values = lax.scan(advance, initial, (decays, driving))  143 us
    dynamic_update_slice x64, other arithmetic, advance(): values = lax.dynamic_update_index_in_dim(values, current, place, 1)  125 us
    dynamic_update_slice x64, other arithmetic, advance(): values = lax.dynamic_update_index_in_dim(values, value, place, 1)  108 us
    mul x64, other arithmetic, advance(): current = factor * value  76.4 us
    select_n x48, other arithmetic, lap(): return jax.tree.map(lambda a, b: jnp.where(reached, a, b), new, before)  76.4 us
    psum x1, blocking collectives, shards(): grad_decay = lax.psum(partial_sum, ('row', 'col')) * decay_rate  64.6 us
    mul x32, other arithmetic, retreat(): return (factor * adjoint, adjoint)  49.2 us
    dot_general x1, other arithmetic, shards(): jnp.einsum('hwnd,hwd->nd', exponent_grad, step_size, precision=highest)  34.8 us
  transfers between devices with their start and end apart: 6, of which 1 were waited for; matrix products, arithmetic and copies ran while one was open for 48% of the time, Pallas kernels for 0%

commit v1 on v0

v1 whole, which is shorter than its diff:
```python
import functools
import math
import jax
import jax.numpy as jnp
from jax import lax
from jax.experimental import pallas as pl
from jax.experimental.pallas import tpu as pltpu
from jax.sharding import PartitionSpec as P

NS = 16
D = 128
S = 8
F32 = jnp.float32
LOG2E = math.log2(math.e)
LN2 = math.log(2.0)
MESH = pl.DeviceIdType.MESH
VMEM = pl.BlockSpec(memory_space=pltpu.VMEM)


def column(ref, h, k, width):
    return ref[h, pl.ds(k, S, stride=width), :]


def spread(block, n):
    return jnp.broadcast_to(block[:, n : n + 1], (S, D))


def set_rates(decay_log, rates):
    for n in range(NS):
        rates[n] = jnp.broadcast_to(-jnp.exp(decay_log[n : n + 1, :]) * LOG2E, (S, D))


def sublane():
    return lax.broadcasted_iota(jnp.int32, (S, D), 0)


def sums_down(value, at):
    for shift in (1, 2, 4):
        value = value + jnp.where(at >= shift, pltpu.roll(value, shift, 0), 0.0)
    return value


def sums_up(value, at):
    for shift in (1, 2, 4):
        value = value + jnp.where(at < S - shift, pltpu.roll(value, S - shift, 0), 0.0)
    return value


def first_kernel(feat, step, write, read, grad, decay_log,
                 leave_v, sum_rows, leave_a, sum_cols, before, later, rates):
    rows, cols = step.shape[0], step.shape[1]
    K = cols // S
    set_rates(decay_log, rates)
    leave_v[...] = jnp.zeros_like(leave_v)
    sum_rows[...] = jnp.zeros_like(sum_rows)
    at = sublane()

    def row(h, carry):
        a = [jnp.zeros((S, D), F32)] * NS
        total = jnp.zeros((S, D), F32)
        for k in reversed(range(K)):
            dt = column(step, h, k, K)
            u = dt * column(feat, h, k, K)
            og = column(grad, h, k, K)
            wb = column(write, h, k, K)
            rb = column(read, h, k, K)
            total = total + dt
            sum_rows[k] += dt
            for n in range(NS):
                e = jnp.exp2(dt * rates[n])
                leave_v[k, n] = e * leave_v[k, n] + u * spread(wb, n)
                a[n] = e * (a[n] + spread(rb, n) * og)
        upto = sums_down(total, at)
        ahead = upto - total
        before[h] = ahead
        sum_cols[h] = upto[S - 1 :, :]
        for n in range(NS):
            m = jnp.exp2(rates[n] * ahead) * a[n]
            z = sums_up(m, at)
            leave_a[h, n : n + 1, :] = z[0:1, :]
            later[h, n] = z - m
        return carry

    lax.fori_loop(0, rows, row, 0)


def second_kernel(feat, step, write, read, grad, decay_log, from_above, from_right,
                  sum_cols, before, later, leave_s, earlier, leave_p, rates, vert):
    rows, cols = step.shape[0], step.shape[1]
    K = cols // S
    set_rates(decay_log, rates)
    vert[...] = from_above[...]
    leave_p[...] = jnp.zeros_like(leave_p)
    at = sublane()
    slow = -jnp.exp(decay_log[...]) * LOG2E

    def forward(h, carry):
        l = [jnp.zeros((S, D), F32)] * NS
        total = jnp.zeros((S, D), F32)
        for k in range(K):
            dt = column(step, h, k, K)
            u = dt * column(feat, h, k, K)
            wb = column(write, h, k, K)
            total = total + dt
            for n in range(NS):
                e = jnp.exp2(dt * rates[n])
                v = e * vert[k, n] + u * spread(wb, n)
                vert[k, n] = v
                l[n] = e * l[n] + v
        upto = before[h] + total
        whole = jnp.exp2(slow * sum_cols[h])
        for n in range(NS):
            m = jnp.exp2(-rates[n] * upto) * l[n]
            z = sums_down(m, at)
            leave_s[h, n : n + 1, :] = whole[n : n + 1, :] * z[S - 1 :, :]
            earlier[h, n] = z - m
        return carry

    def backward(i, carry):
        h = rows - 1 - i
        total = jnp.zeros((S, D), F32)
        for k in range(K):
            total = total + column(step, h, k, K)
        upto = before[h] + total
        entering = jnp.exp2(slow * sum_cols[h]) * from_right[h]
        a = [
            jnp.exp2(-rates[n] * upto) * (later[h, n] + entering[n : n + 1, :])
            for n in range(NS)
        ]
        for k in reversed(range(K)):
            dt = column(step, h, k, K)
            og = column(grad, h, k, K)
            rb = column(read, h, k, K)
            for n in range(NS):
                e = jnp.exp2(dt * rates[n])
                ah = a[n] + spread(rb, n) * og
                leave_p[k, n] = e * (ah + leave_p[k, n])
                a[n] = e * ah
        return carry

    lax.fori_loop(0, rows, forward, 0)
    lax.fori_loop(0, rows, backward, 0)


def third_kernel(feat, step, write, read, grad, decay_log, from_above, from_right, from_left,
                 from_below, sum_cols, before, later, earlier,
                 g_feat, g_step, g_write, g_read, g_decay, rates, vert, below, kept_s, kept_v):
    rows, cols = step.shape[0], step.shape[1]
    K = cols // S
    set_rates(decay_log, rates)
    vert[...] = from_above[...]
    below[...] = from_below[...]
    g_decay[...] = jnp.zeros_like(g_decay)
    lane = lax.broadcasted_iota(jnp.int32, (S, D), 1)
    slow = -jnp.exp(decay_log[...]) * LOG2E

    def forward(h, carry):
        ahead = before[h]
        s = [
            jnp.exp2(rates[n] * ahead) * (earlier[h, n] + from_left[h, n : n + 1, :])
            for n in range(NS)
        ]
        for k in range(K):
            dt = column(step, h, k, K)
            u = dt * column(feat, h, k, K)
            og = column(grad, h, k, K)
            wb = column(write, h, k, K)
            out = jnp.zeros((S, D), F32)
            for n in range(NS):
                e = jnp.exp2(dt * rates[n])
                q = e * vert[k, n]
                v = q + u * spread(wb, n)
                vert[k, n] = v
                t = e * s[n]
                s[n] = t + v
                kept_v[h, k, n] = q
                kept_s[h, k, n] = t
                out = jnp.where(lane == n, jnp.sum(s[n] * og, axis=1, keepdims=True), out)
            g_read[h, k] = out[:, :NS]
        return carry

    def backward(i, carry):
        h = rows - 1 - i
        total = jnp.zeros((S, D), F32)
        for k in range(K):
            total = total + column(step, h, k, K)
        upto = before[h] + total
        entering = jnp.exp2(slow * sum_cols[h]) * from_right[h]
        a = [
            jnp.exp2(-rates[n] * upto) * (later[h, n] + entering[n : n + 1, :])
            for n in range(NS)
        ]
        for k in reversed(range(K)):
            dt = column(step, h, k, K)
            fx = column(feat, h, k, K)
            u = dt * fx
            og = column(grad, h, k, K)
            wb = column(write, h, k, K)
            rb = column(read, h, k, K)
            out = jnp.zeros((S, D), F32)
            through = jnp.zeros((S, D), F32)
            rated = jnp.zeros((S, D), F32)
            for n in range(NS):
                e = jnp.exp2(dt * rates[n])
                ah = a[n] + spread(rb, n) * og
                av = ah + below[k, n]
                below[k, n] = e * av
                a[n] = e * ah
                eg = ah * kept_s[h, k, n] + av * kept_v[h, k, n]
                through = through + av * spread(wb, n)
                rated = rated + eg * rates[n]
                g_decay[n] += eg * dt
                out = jnp.where(lane == n, jnp.sum(av * u, axis=1, keepdims=True), out)
            g_write[h, k] = out[:, :NS]
            g_feat[h, pl.ds(k, S, stride=K), :] = dt * through
            g_step[h, pl.ds(k, S, stride=K), :] = fx * through + LN2 * rated
        return carry

    lax.fori_loop(0, rows, forward, 0)
    lax.fori_loop(0, rows, backward, 0)


def exchange_kernel(forward_rows, first, nr, nc, *refs):
    if first:
        (leave_r, sum_r, leave_c, sum_c, decay_log, got_r, got_c, sums_r, sums_c,
         in_r, in_c, out_r, out_c, s_out, s_in, b_out, b_in, q_out, q_in) = refs
    else:
        (leave_r, sums_r, leave_c, sums_c, decay_log, got_r, got_c,
         in_r, in_c, out_r, out_c, s_out, s_in, b_out, b_in) = refs
    ri, ci = lax.axis_index("row"), lax.axis_index("col")
    kr = leave_r.shape[0] // nr
    hc = leave_c.shape[0] // nc
    barrier = pltpu.get_barrier_semaphore()
    row_peers = [(lax.rem(ri + o, nr), ci) for o in range(1, nr)]
    col_peers = [(ri, lax.rem(ci + o, nc)) for o in range(1, nc)]
    for peer in row_peers + col_peers:
        pl.semaphore_signal(barrier, inc=1, device_id=peer, device_id_type=MESH)
    pl.semaphore_wait(barrier, len(row_peers) + len(col_peers))

    def send(src, dst, out_sem, in_sem, at, peer):
        copy = pltpu.make_async_remote_copy(
            src_ref=src, dst_ref=dst, send_sem=out_sem.at[at], recv_sem=in_sem.at[at],
            device_id=peer, device_id_type=MESH)
        copy.start()
        return copy

    copies = []
    for o, peer in enumerate(row_peers):
        src = leave_r.at[pl.ds(peer[0] * kr, kr)]
        copies.append(send(src, in_r.at[ri], s_out, s_in, o, peer))
        if first:
            src = sum_r.at[pl.ds(peer[0] * kr, kr)]
            copies.append(send(src, sums_r.at[ri], q_out, q_in, o, peer))
    for o, peer in enumerate(col_peers):
        src = leave_c.at[pl.ds(peer[1] * hc, hc)]
        copies.append(send(src, in_c.at[ci], s_out, s_in, nr - 1 + o, peer))
        if first:
            src = sum_c.at[pl.ds(peer[1] * hc, hc)]
            copies.append(send(src, sums_c.at[ci], q_out, q_in, nr - 1 + o, peer))
    in_r[ri] = leave_r[pl.ds(ri * kr, kr)]
    in_c[ci] = leave_c[pl.ds(ci * hc, hc)]
    if first:
        sums_r[ri] = sum_r[pl.ds(ri * kr, kr)]
        sums_c[ci] = sum_c[pl.ds(ci * hc, hc)]
    for copy in copies:
        copy.wait()
    rate = -jnp.exp(decay_log[...]) * LOG2E

    for j in range(hc):
        now = jnp.zeros((NS, D), F32)
        for c in (reversed(range(nc)) if forward_rows else range(nc)):
            out_c[c, j] = now
            now = jnp.exp2(rate * sums_c[c, j]) * now + in_c[c, j]

    def scan_row(i, carry):
        for j in range(kr):
            r2 = -jnp.exp(decay_log[pl.ds(i, 1), :]) * LOG2E
            now = jnp.zeros((S, D), F32)
            for r in (range(nr) if forward_rows else reversed(range(nr))):
                out_r[r, j, i] = now
                now = jnp.exp2(r2 * sums_r[r, j]) * now + in_r[r, j, i]
        return carry

    back = []
    for o, peer in enumerate(col_peers):
        back.append(send(out_c.at[peer[1]], got_c.at[pl.ds(ci * hc, hc)], b_out, b_in,
                         nr - 1 + o, peer))
    lax.fori_loop(0, NS, scan_row, 0)
    for o, peer in enumerate(row_peers):
        back.append(send(out_r.at[peer[0]], got_r.at[pl.ds(ri * kr, kr)], b_out, b_in, o, peer))
    got_c[pl.ds(ci * hc, hc)] = out_c[ci]
    got_r[pl.ds(ri * kr, kr)] = out_r[ri]
    for copy in back:
        copy.wait()


def exchange(forward_rows, first, nr, nc, leave_r, sum_r, leave_c, sum_c, decay_log):
    K, rows = leave_r.shape[0], leave_c.shape[0]
    kr, hc = K // nr, rows // nc
    peers = nr + nc - 2
    sds = jax.ShapeDtypeStruct
    outs = [sds(leave_r.shape, F32), sds(leave_c.shape, F32)]
    if first:
        outs += [sds((nr, kr, S, D), F32), sds((nc, hc, 1, D), F32)]
    dma = pltpu.SemaphoreType.DMA((peers,))
    return pl.pallas_call(
        functools.partial(exchange_kernel, forward_rows, first, nr, nc),
        out_shape=outs,
        in_specs=[VMEM] * 5,
        out_specs=[VMEM] * len(outs),
        scratch_shapes=[
            pltpu.VMEM((nr, kr, NS, S, D), F32),
            pltpu.VMEM((nc, hc, NS, D), F32),
            pltpu.VMEM((nr, kr, NS, S, D), F32),
            pltpu.VMEM((nc, hc, NS, D), F32),
        ] + [dma] * (6 if first else 4),
        compiler_params=pltpu.CompilerParams(
            collective_id=0 if first else 1, has_side_effects=True,
            vmem_limit_bytes=16 << 20),
        name="exchange_first" if first else "exchange_second",
    )(leave_r, sum_r, leave_c, sum_c, decay_log)


def shards(features, step_size, write_weights, read_weights, decay_log, out_grad):
    rows, cols = step_size.shape[0], step_size.shape[1]
    K = cols // S
    nr, nc = lax.axis_size("row"), lax.axis_size("col")
    sds = jax.ShapeDtypeStruct
    raw = (features, step_size, write_weights, read_weights, out_grad, decay_log)
    carry_r, carry_c = (K, NS, S, D), (rows, NS, D)
    rates = pltpu.VMEM((NS, S, D), F32)

    def call(kernel, outs, scratch, args, limit):
        return pl.pallas_call(
            kernel,
            out_shape=[sds(o, F32) for o in outs],
            in_specs=[VMEM] * len(args),
            out_specs=[VMEM] * len(outs),
            scratch_shapes=scratch,
            compiler_params=pltpu.CompilerParams(vmem_limit_bytes=limit << 20),
        )(*args)

    leave_v, sum_rows, leave_a, sum_cols, before, later = call(
        first_kernel,
        [carry_r, (K, S, D), carry_c, (rows, 1, D), (rows, S, D), (rows, NS, S, D)],
        [rates], raw, 24)
    from_above, from_right, sums_r, sums_c = exchange(
        True, True, nr, nc, leave_v, sum_rows, leave_a, sum_cols, decay_log)
    leave_s, earlier, leave_p = call(
        second_kernel,
        [carry_c, (rows, NS, S, D), carry_r],
        [rates, pltpu.VMEM(carry_r, F32)],
        raw + (from_above, from_right, sum_cols, before, later), 24)
    from_below, from_left = exchange(
        False, False, nr, nc, leave_p, sums_r, leave_s, sums_c, decay_log)
    g_feat, g_step, g_write, g_read, g_decay = call(
        third_kernel,
        [(rows, cols, D), (rows, cols, D), (rows, K, S, NS), (rows, K, S, NS), (NS, S, D)],
        [rates, pltpu.VMEM(carry_r, F32), pltpu.VMEM(carry_r, F32),
         pltpu.VMEM((rows, K, NS, S, D), F32), pltpu.VMEM((rows, K, NS, S, D), F32)],
        raw + (from_above, from_right, from_left, from_below, sum_cols, before, later, earlier),
        58)

    def as_columns(g):
        return g.transpose(0, 2, 1, 3).reshape(rows, cols, NS)

    rate = -jnp.exp(decay_log)
    g_decay = lax.psum(jnp.sum(g_decay, axis=1), ("row", "col")) * rate
    return (g_feat, g_step, as_columns(g_write), as_columns(g_read), g_decay)


def solution(mesh):
    tiles = P("row", "col", None)
    in_specs = (tiles, tiles, tiles, tiles, P(), tiles)
    out_specs = (tiles, tiles, tiles, tiles, P())
    return jax.shard_map(shards, mesh=mesh, in_specs=in_specs, out_specs=out_specs, check_vma=False)
```

time: 984 us -> 390 us (0.40); the launches traced: 968 us -> 389 us
  other arithmetic: 690 us -> 1.56 us
  Pallas kernels: 0 us -> 312 us
  local copies, waits for them, and re-layouts: 98.4 us -> 12.5 us
  matrix products: 74.7 us -> 0 us
  waiting for transfers between devices: 23 us -> 0 us
  between operations: 14.6 us -> 0.85 us
    dynamic_update_slice x192 -> x0, other arithmetic: 376 us -> none  [the longest x64 143 us: sweep_rows(): closing, values = lax.scan(advance, initial, (decays, driving))]
    pallas_call x0 -> x5, Pallas kernels: none -> 312 us  [the longest x3 265 us: call(): pl.pallas_call(kernel, out_shape=[sds(o, F32) for o in outs], in_specs=[V...]
    mul x100 -> x1, other arithmetic: 147 us -> 0.61 us  [shards(): g_decay = lax.psum(jnp.sum(g_decay, axis=1), ('row', 'col')) * rate]
    select_n x48 -> x0, other arithmetic: 76.4 us -> none  [lap(): return jax.tree.map(lambda a, b: jnp.where(reached, a, b), new, before)]
    dot_general x3 -> x0, matrix products: 74.7 us -> none  [the longest x1 28.9 us: shards(): jnp.einsum('hwnd,hwd->hwn', adjoint_v, step_size * features, precision=hi...]
    add x2 -> x0, other arithmetic: 35.4 us -> none  [the longest x1 23.2 us: shards(): local_cols + jnp.exp(running_cols[:, :, None, :] * decay_rate) * from_lef...]
    dot_general x1 -> x0, other arithmetic: 34.8 us -> none  [shards(): jnp.einsum('hwnd,hwd->nd', exponent_grad, step_size, precision=highest)]
    another operation x5 -> x0, local copies, waits for them, and re-layouts: 33.3 us -> none
  transfers between devices with their start and end apart: 6 -> 0, of which waited for: 1 -> 0; matrix products, arithmetic and copies ran while one was open for 48% -> 0% of each run, Pallas kernels for 0% -> 0%
where the time goes in v1:
time: 390 us; the launch traced here: 389 us
  Pallas kernels  312 us (80%)
  blocking collectives  62.8 us (16%)
  local copies, waits for them, and re-layouts  12.5 us (3%)
    pallas_call x3, Pallas kernels, call(): pl.pallas_call(kernel, out_shape=[sds(o, F32) for o in outs], in_specs=[V...  265 us
    psum x1, blocking collectives, shards(): g_decay = lax.psum(jnp.sum(g_decay, axis=1), ('row', 'col')) * rate  62.8 us
    pallas_call x2, Pallas kernels, exchange(): pl.pallas_call(functools.partial(exchange_kernel, forward_rows, first, nr...  46.3 us
    unnamed x36, local copies, waits for them, and re-layouts  10.1 us

profile of v1, /device:TPU:1, one launch (start us, length us, event | category | flops | bytes accessed | tf_op | source)
XLA Modules:
  0.0 389.5 jit_solution(11477257895118514712)
XLA Ops:
  0.6 0.0 copy-start.11
  0.6 0.0 copy-start.2
  0.7 1.4 copy.21.write
  2.0 0.0 copy-start
  2.1 1.5 copy.22.read
  3.5 0.0 copy-done.11
  3.5 0.0 copy-done.2
  3.5 0.0 copy-start.3
  3.6 1.2 copy-done.3
  4.8 0.0 copy-start.4
  4.8 1.2 copy-done.4
  6.0 0.0 copy-start.1
  6.0 16.1 %shard_map.101 = (f32[8,16,8,128]{3,2,1,0:T(8,128)S(1)}, f32[8,8,128]{2,1,0:T(8,128)S(1)}, f32[32,16,128]{2,1,0:T(8,128)S(1)}, f32[32,1,128]{2,1,0:T(1,128)S(1)}...) custom-call(f32[32,64,128]{2,1,0:T(8,128)S(1)} %copy-done.2, f32[32,64,128]{2,1,0:T(8,128)S(1)} %copy-done.3, ...), custom_call_target="tpu_custom_call" | custom-call | tf_op jit(solution)/shard_map/pallas_call | solution.py:334
  22.1 0.0 copy-start.5
  22.1 0.0 copy-start.9
  22.1 0.0 copy-start.14
  22.1 26.7 %exchange_first.1 = (f32[8,16,8,128]{3,2,1,0:T(8,128)S(1)}, f32[32,16,128]{2,1,0:T(8,128)S(1)}, f32[8,1,8,128]{3,2,1,0:T(8,128)S(1)}, f32[16,2,1,128]{3,2,1,0:T(1,128)S(1)}) custom-call(f32[8,16,8,128]{3,2,1,0:T(8,128)S(1)} %get-tuple-element.25.refs_0_, f32[8,8,128]{2,1,0:T(8,128)S(1)} %get-tuple-element.26.refs_1_, ...), custom_call_target="tpu_custom_call" | custom-call | tf_op jit(solution)/shard_map/exchange_first/pallas_call | solution.py:306
  48.8 0.0 copy-start.6
  48.9 0.0 copy-start.8
  48.9 0.0 copy-done
  48.9 0.0 copy-done.1
  48.9 19.5 %shard_map.102 = (f32[32,16,128]{2,1,0:T(8,128)S(1)}, f32[32,16,8,128]{3,2,1,0:T(8,128)S(1)}, f32[8,16,8,128]{3,2,1,0:T(8,128)S(1)}) custom-call(f32[32,64,128]{2,1,0:T(8,128)S(1)} %copy-done.2, f32[32,64,128]{2,1,0:T(8,128)S(1)} %copy-done.3, f32[32,64,16]{2,1,0:T(8,128)S(1)} %copy.21.write, f32[32,64,16]{2,1,0:T(8,128)S(1)} %copy.22.read, ...), custom_call_target="tpu_custom_call" | custom-call | tf_op jit(solution)/shard_map/pallas_call | solution.py:334
  68.3 0.0 copy-done.5
  68.4 0.0 copy-done.9
  68.4 0.0 copy-done.14
  68.4 0.0 copy-done.6
  68.4 0.0 copy-done.8
  68.4 0.0 copy-start.7
  68.4 1.3 copy-done.7
  69.7 19.7 %exchange_second.1 = (f32[8,16,8,128]{3,2,1,0:T(8,128)S(1)}, f32[32,16,128]{2,1,0:T(8,128)S(1)}) custom-call(f32[8,16,8,128]{3,2,1,0:T(8,128)S(1)} %get-tuple-element.33.refs_0_, f32[8,1,8,128]{3,2,1,0:T(8,128)S(1)} %get-tuple-element.34.refs_1_, f32[32,16,128]{2,1,0:T(8,128)S(1)} %get-tuple-element.35.refs_2_, ...), custom_call_target="tpu_custom_call" | custom-call | tf_op jit(solution)/shard_map/exchange_second/pallas_call | solution.py:306
  89.4 0.0 copy-start.10
  89.4 0.8 copy-done.10
  90.2 0.0 copy-start.13
  90.2 0.7 copy-done.13
  90.9 0.0 copy-start.12
  90.9 229.9 %shard_map.103 = (f32[32,64,128]{2,1,0:T(8,128)}, f32[32,64,128]{2,1,0:T(8,128)}, f32[32,8,8,16]{3,2,1,0:T(8,128)}, f32[32,8,8,16]{3,2,1,0:T(8,128)}, f32[16,8,128]{2,1,0:T(8,128)}) custom-call(f32[32,64,128]{2,1,0:T(8,128)} %feat.5, f32[32,64,128]{2,1,0:T(8,128)} %step.5, f32[32,64,16]{2,1,0:T(8,128)} %copy-done, f32[32,64,16]{2,1,0:T(8,128)} %copy-done.1, ...), custom_call_target="tpu_custom_call" | custom-call | tf_op jit(solution)/shard_map/pallas_call | solution.py:334
  320.8 0.0 copy-start.15
  320.8 0.9 reduce_sum.9
  321.7 62.8 %psum.7 = f32[16,128]{1,0:T(8,128)S(1)} all-reduce(f32[16,128]{1,0:T(8,128)S(1)} %reduce_sum.9), channel_id=1, replica_groups=mesh['row'=8,'col'=16] {'row','col'}, use_global_device_ids=true, to_apply=%region_1.0 | all-reduce | flops 2048 | bytes 16384 | tf_op jit(solution)/shard_map/psum | solution.py:368
  384.6 0.0 copy-done.12
  384.6 0.6 negate_multiply_fusion
  385.2 1.7 copy.23
  386.9 1.0 copy.25
  387.9 0.0 copy-done.15
  387.9 0.6 copy.24
  388.5 1.0 copy.26
Async XLA Ops:
  0.6 2.9 copy-start.11
  0.6 2.9 copy-start.2
  2.0 46.8 %copy-start = (f32[32,64,16]{2,1,0:T(8,128)}, f32[32,64,16]{2,1,0:T(8,128)S(1)}, u32[]{:S(2)}) copy-start(f32[32,64,16]{2,1,0:T(8,128)S(1)} %copy.21.write) | copy-start | bytes 393220
  3.5 1.2 copy-start.3
  4.8 1.2 copy-start.4
  6.0 42.9 %copy-start.1 = (f32[32,64,16]{2,1,0:T(8,128)}, f32[32,64,16]{2,1,0:T(8,128)S(1)}, u32[]{:S(2)}) copy-start(f32[32,64,16]{2,1,0:T(8,128)S(1)} %copy.22.read) | copy-start | bytes 393220
  22.1 46.2 %copy-start.5 = (f32[32,16,8,128]{3,2,1,0:T(8,128)}, f32[32,16,8,128]{3,2,1,0:T(8,128)S(1)}, u32[]{:S(2)}) copy-start(f32[32,16,8,128]{3,2,1,0:T(8,128)S(1)} %get-tuple-element.32.later) | copy-start | bytes 6291460
  22.1 46.2 %copy-start.9 = (f32[32,8,128]{2,1,0:T(8,128)}, f32[32,8,128]{2,1,0:T(8,128)S(1)}, u32[]{:S(2)}) copy-start(f32[32,8,128]{2,1,0:T(8,128)S(1)} %get-tuple-element.31.before) | copy-start | bytes 393220
  22.1 46.2 %copy-start.14 = (f32[32,1,128]{2,1,0:T(1,128)}, f32[32,1,128]{2,1,0:T(1,128)S(1)}, u32[]{:S(2)}) copy-start(f32[32,1,128]{2,1,0:T(1,128)S(1)} %get-tuple-element.28.refs_3_.sum_cols) | copy-start | bytes 49156
  48.8 19.5 %copy-start.6 = (f32[8,16,8,128]{3,2,1,0:T(8,128)}, f32[8,16,8,128]{3,2,1,0:T(8,128)S(1)}, u32[]{:S(2)}) copy-start(f32[8,16,8,128]{3,2,1,0:T(8,128)S(1)} %get-tuple-element.29.from_above) | copy-start | bytes 1572868
  48.9 19.5 %copy-start.8 = (f32[32,16,128]{2,1,0:T(8,128)}, f32[32,16,128]{2,1,0:T(8,128)S(1)}, u32[]{:S(2)}) copy-start(f32[32,16,128]{2,1,0:T(8,128)S(1)} %get-tuple-element.30.from_right) | copy-start | bytes 786436
  68.4 1.3 copy-start.7
  89.4 0.8 copy-start.10
  90.2 0.7 copy-start.13
  90.9 293.7 %copy-start.12 = (f32[16,128]{1,0:T(8,128)S(1)}, f32[16,128]{1,0:T(8,128)}, u32[]{:S(2)}) copy-start(f32[16,128]{1,0:T(8,128)} %decay_log.5) | copy-start | bytes 24580
  320.8 67.1 %copy-start.15 = (f32[32,8,8,16]{3,2,1,0:T(8,128)S(1)}, f32[32,8,8,16]{3,2,1,0:T(8,128)}, u32[]{:S(2)}) copy-start(f32[32,8,8,16]{3,2,1,0:T(8,128)} %get-tuple-element.43) | copy-start | bytes 393220

commit v2 on v1

--- a/solution.py
+++ b/solution.py
@@ -44,6 +44,22 @@
     for shift in (1, 2, 4):
         value = value + jnp.where(at < S - shift, pltpu.roll(value, S - shift, 0), 0.0)
     return value
+
+
+def set_selector(selector):
+    of = lax.broadcasted_iota(jnp.int32, selector.shape, 0) // D
+    to = lax.broadcasted_iota(jnp.int32, selector.shape, 1)
+    selector[...] = jnp.where(of == to, 1.0, 0.0).astype(jnp.bfloat16)
+
+
+def channel_sums(products, selector):
+    values = products[...]
+    high = values.astype(jnp.bfloat16)
+    low = (values - high.astype(F32)).astype(jnp.bfloat16)
+    both = jnp.concatenate([high, low], axis=0)
+    sums = jnp.dot(both, selector[...], preferred_element_type=F32)
+    size = values.shape[0]
+    return (sums[:size] + sums[size:])[:, :NS]
 
 
 def first_kernel(feat, step, write, read, grad, decay_log,
@@ -144,14 +160,14 @@
 
 def third_kernel(feat, step, write, read, grad, decay_log, from_above, from_right, from_left,
                  from_below, sum_cols, before, later, earlier,
-                 g_feat, g_step, g_write, g_read, g_decay, rates, vert, below, kept_s, kept_v):
+                 g_feat, g_step, g_write, g_read, g_decay, rates, vert, below, kept_s, kept_v, products, selector):
     rows, cols = step.shape[0], step.shape[1]
     K = cols // S
     set_rates(decay_log, rates)
     vert[...] = from_above[...]
     below[...] = from_below[...]
     g_decay[...] = jnp.zeros_like(g_decay)
-    lane = lax.broadcasted_iota(jnp.int32, (S, D), 1)
+    set_selector(selector)
     slow = -jnp.exp(decay_log[...]) * LOG2E
 
     def forward(h, carry):
@@ -165,7 +181,6 @@
             u = dt * column(feat, h, k, K)
             og = column(grad, h, k, K)
             wb = column(write, h, k, K)
-            out = jnp.zeros((S, D), F32)
             for n in range(NS):
                 e = jnp.exp2(dt * rates[n])
                 q = e * vert[k, n]
@@ -175,8 +190,8 @@
                 s[n] = t + v
                 kept_v[h, k, n] = q
                 kept_s[h, k, n] = t
-                out = jnp.where(lane == n, jnp.sum(s[n] * og, axis=1, keepdims=True), out)
-            g_read[h, k] = out[:, :NS]
+                products[S * k : S * k + S, D * n : D * n + D] = s[n] * og
+        g_read[h] = channel_sums(products, selector)
         return carry
 
     def backward(i, carry):
@@ -197,7 +212,6 @@
             og = column(grad, h, k, K)
             wb = column(write, h, k, K)
             rb = column(read, h, k, K)
-            out = jnp.zeros((S, D), F32)
             through = jnp.zeros((S, D), F32)
             rated = jnp.zeros((S, D), F32)
             for n in range(NS):
@@ -210,10 +224,10 @@
                 through = through + av * spread(wb, n)
                 rated = rated + eg * rates[n]
                 g_decay[n] += eg * dt
-                out = jnp.where(lane == n, jnp.sum(av * u, axis=1, keepdims=True), out)
-            g_write[h, k] = out[:, :NS]
+                products[S * k : S * k + S, D * n : D * n + D] = av * u
             g_feat[h, pl.ds(k, S, stride=K), :] = dt * through
             g_step[h, pl.ds(k, S, stride=K), :] = fx * through + LN2 * rated
+        g_write[h] = channel_sums(products, selector)
         return carry
 
     lax.fori_loop(0, rows, forward, 0)
@@ -321,6 +335,47 @@
     )(leave_r, sum_r, leave_c, sum_c, decay_log)
 
 
+def total_kernel(nr, nc, part, decay_log, out, by_row, by_col, s_out, s_in):
+    ri, ci = lax.axis_index("row"), lax.axis_index("col")
+    row_peers = [(lax.rem(ri + o, nr), ci) for o in range(1, nr)]
+    col_peers = [(ri, lax.rem(ci + o, nc)) for o in range(1, nc)]
+    barrier = pltpu.get_barrier_semaphore()
+    for peer in row_peers + col_peers:
+        pl.semaphore_signal(barrier, inc=1, device_id=peer, device_id_type=MESH)
+    pl.semaphore_wait(barrier, len(row_peers) + len(col_peers))
+
+    def stage(value, box, mine, peers, base):
+        box[mine] = value
+        copies = []
+        for o, peer in enumerate(peers):
+            copy = pltpu.make_async_remote_copy(
+                src_ref=box.at[mine], dst_ref=box.at[mine], send_sem=s_out.at[base + o],
+                recv_sem=s_in.at[base + o], device_id=peer, device_id_type=MESH)
+            copy.start()
+            copies.append(copy)
+        for copy in copies:
+            copy.wait()
+        return jnp.sum(box[...], axis=0)
+
+    value = stage(jnp.sum(part[...], axis=1), by_row, ri, row_peers, 0)
+    value = stage(value, by_col, ci, col_peers, nr - 1)
+    out[...] = value * -jnp.exp(decay_log[...])
+
+
+def total(nr, nc, part, decay_log):
+    dma = pltpu.SemaphoreType.DMA((nr + nc - 2,))
+    return pl.pallas_call(
+        functools.partial(total_kernel, nr, nc),
+        out_shape=jax.ShapeDtypeStruct((NS, D), F32),
+        in_specs=[VMEM] * 2,
+        out_specs=VMEM,
+        scratch_shapes=[pltpu.VMEM((nr, NS, D), F32), pltpu.VMEM((nc, NS, D), F32), dma, dma],
+        compiler_params=pltpu.CompilerParams(
+            collective_id=2, has_side_effects=True, vmem_limit_bytes=4 << 20),
+        name="total",
+    )(part, decay_log)
+
+
 def shards(features, step_size, write_weights, read_weights, decay_log, out_grad):
     rows, cols = step_size.shape[0], step_size.shape[1]
     K = cols // S
@@ -355,17 +410,17 @@
         False, False, nr, nc, leave_p, sums_r, leave_s, sums_c, decay_log)
     g_feat, g_step, g_write, g_read, g_decay = call(
         third_kernel,
-        [(rows, cols, D), (rows, cols, D), (rows, K, S, NS), (rows, K, S, NS), (NS, S, D)],
+        [(rows, cols, D), (rows, cols, D), (rows, cols, NS), (rows, cols, NS), (NS, S, D)],
         [rates, pltpu.VMEM(carry_r, F32), pltpu.VMEM(carry_r, F32),
-         pltpu.VMEM((rows, K, NS, S, D), F32), pltpu.VMEM((rows, K, NS, S, D), F32)],
+         pltpu.VMEM((rows, K, NS, S, D), F32), pltpu.VMEM((rows, K, NS, S, D), F32),
+         pltpu.VMEM((cols, NS * D), F32), pltpu.VMEM((NS * D, D), jnp.bfloat16)],
         raw + (from_above, from_right, from_left, from_below, sum_cols, before, later, earlier),
         58)
 
     def as_columns(g):
-        return g.transpose(0, 2, 1, 3).reshape(rows, cols, NS)
-
-    rate = -jnp.exp(decay_log)
-    g_decay = lax.psum(jnp.sum(g_decay, axis=1), ("row", "col")) * rate
+        return g.reshape(rows, K, S, NS).transpose(0, 2, 1, 3).reshape(rows, cols, NS)
+
+    g_decay = total(nr, nc, g_decay, decay_log)
     return (g_feat, g_step, as_columns(g_write), as_columns(g_read), g_decay)
 
 

time: 390 us -> 149 us (0.38)
  Pallas kernels: 312 us -> 134 us
  blocking collectives: 62.8 us -> 0 us
    pallas_call x3, Pallas kernels: 265 us -> 77.3 us  [call(): pl.pallas_call(kernel, out_shape=[sds(o, F32) for o in outs], in_specs=[V...]
    psum x1 -> x0, blocking collectives: 62.8 us -> none  [shards(): g_decay = lax.psum(jnp.sum(g_decay, axis=1), ('row', 'col')) * rate]
    pallas_call x0 -> x1, Pallas kernels: none -> 10.5 us  [total(): pl.pallas_call(functools.partial(total_kernel, nr, nc), out_shape=jax.Sha...]
    unnamed x36 -> x39, local copies, waits for them, and re-layouts: 10.1 us -> 11.6 us
where the time goes in v2:
time: 149 us
  Pallas kernels  134 us (90%)
  local copies, waits for them, and re-layouts  13.9 us (9%)
    pallas_call x3, Pallas kernels, call(): pl.pallas_call(kernel, out_shape=[sds(o, F32) for o in outs], in_specs=[V...  77.3 us
    pallas_call x2, Pallas kernels, exchange(): pl.pallas_call(functools.partial(exchange_kernel, forward_rows, first, nr...  46.4 us
    unnamed x39, local copies, waits for them, and re-layouts  11.6 us
    pallas_call x1, Pallas kernels, total(): pl.pallas_call(functools.partial(total_kernel, nr, nc), out_shape=jax.Sha...  10.5 us

profile of v2, /device:TPU:1, one launch (start us, length us, event | category | flops | bytes accessed | tf_op | source)
XLA Modules:
  0.0 149.0 jit_solution(17917458502066704404)
XLA Ops:
  0.6 0.0 copy-start.11
  0.6 0.0 copy-start.2
  0.7 1.4 copy.23.write
  2.0 0.0 copy-start
  2.1 1.5 copy.24.read
  3.5 0.0 copy-done.11
  3.5 0.0 copy-done.2
  3.5 0.0 copy-start.3
  3.6 1.2 copy-done.3
  4.8 0.0 copy-start.4
  4.8 1.2 copy-done.4
  6.0 0.0 copy-start.1
  6.0 16.1 %shard_map.101 = (f32[8,16,8,128]{3,2,1,0:T(8,128)S(1)}, f32[8,8,128]{2,1,0:T(8,128)S(1)}, f32[32,16,128]{2,1,0:T(8,128)S(1)}, f32[32,1,128]{2,1,0:T(1,128)S(1)}...) custom-call(f32[32,64,128]{2,1,0:T(8,128)S(1)} %copy-done.2, f32[32,64,128]{2,1,0:T(8,128)S(1)} %copy-done.3, ...), custom_call_target="tpu_custom_call" | custom-call | tf_op jit(solution)/shard_map/pallas_call | solution.py:389
  22.1 0.0 copy-start.5
  22.1 0.0 copy-start.9
  22.1 0.0 copy-start.14
  22.1 26.7 %exchange_first.1 = (f32[8,16,8,128]{3,2,1,0:T(8,128)S(1)}, f32[32,16,128]{2,1,0:T(8,128)S(1)}, f32[8,1,8,128]{3,2,1,0:T(8,128)S(1)}, f32[16,2,1,128]{3,2,1,0:T(1,128)S(1)}) custom-call(f32[8,16,8,128]{3,2,1,0:T(8,128)S(1)} %get-tuple-element.25.refs_0_, f32[8,8,128]{2,1,0:T(8,128)S(1)} %get-tuple-element.26.refs_1_, ...), custom_call_target="tpu_custom_call" | custom-call | tf_op jit(solution)/shard_map/exchange_first/pallas_call | solution.py:320
  48.8 0.0 copy-start.6
  48.9 0.0 copy-start.8
  48.9 0.0 copy-done
  48.9 0.0 copy-done.1
  48.9 19.5 %shard_map.102 = (f32[32,16,128]{2,1,0:T(8,128)S(1)}, f32[32,16,8,128]{3,2,1,0:T(8,128)S(1)}, f32[8,16,8,128]{3,2,1,0:T(8,128)S(1)}) custom-call(f32[32,64,128]{2,1,0:T(8,128)S(1)} %copy-done.2, f32[32,64,128]{2,1,0:T(8,128)S(1)} %copy-done.3, f32[32,64,16]{2,1,0:T(8,128)S(1)} %copy.23.write, f32[32,64,16]{2,1,0:T(8,128)S(1)} %copy.24.read, ...), custom_call_target="tpu_custom_call" | custom-call | tf_op jit(solution)/shard_map/pallas_call | solution.py:389
  68.3 0.0 copy-done.5
  68.4 0.0 copy-done.9
  68.4 0.0 copy-done.14
  68.4 0.0 copy-done.6
  68.4 0.0 copy-done.8
  68.4 0.0 copy-start.7
  68.4 1.3 copy-done.7
  69.7 19.7 %exchange_second.1 = (f32[8,16,8,128]{3,2,1,0:T(8,128)S(1)}, f32[32,16,128]{2,1,0:T(8,128)S(1)}) custom-call(f32[8,16,8,128]{3,2,1,0:T(8,128)S(1)} %get-tuple-element.33.refs_0_, f32[8,1,8,128]{3,2,1,0:T(8,128)S(1)} %get-tuple-element.34.refs_1_, f32[32,16,128]{2,1,0:T(8,128)S(1)} %get-tuple-element.35.refs_2_, ...), custom_call_target="tpu_custom_call" | custom-call | tf_op jit(solution)/shard_map/exchange_second/pallas_call | solution.py:320
  89.4 0.0 copy-start.10
  89.4 0.8 copy-done.10
  90.2 0.0 copy-start.13
  90.2 0.7 copy-done.13
  90.9 0.0 copy-start.12
  90.9 41.7 %shard_map.103 = (f32[32,64,128]{2,1,0:T(8,128)}, f32[32,64,128]{2,1,0:T(8,128)}, f32[32,64,16]{2,1,0:T(8,128)}, f32[32,64,16]{2,1,0:T(8,128)}, f32[16,8,128]{2,1,0:T(8,128)}) custom-call(f32[32,64,128]{2,1,0:T(8,128)} %feat.5, f32[32,64,128]{2,1,0:T(8,128)} %step.5, f32[32,64,16]{2,1,0:T(8,128)} %copy-done, f32[32,64,16]{2,1,0:T(8,128)} %copy-done.1, ...), custom_call_target="tpu_custom_call" | custom-call | tf_op jit(solution)/shard_map/pallas_call | solution.py:389
  132.6 0.0 copy-done.12
  132.6 0.0 copy-start.15
  132.7 0.8 copy-done.15
  133.5 0.0 copy-start.16
  133.5 10.5 %total.1 = f32[16,128]{1,0:T(8,128)S(1)} custom-call(f32[16,8,128]{2,1,0:T(8,128)S(1)} %copy-done.15, f32[16,128]{1,0:T(8,128)S(1)} %copy-done.12), custom_call_target="tpu_custom_call" | custom-call | tf_op jit(solution)/shard_map/total/pallas_call | solution.py:367
  144.0 1.7 %copy.25 = f32[32,8,8,16]{0,3,1,2:T(8,128)S(1)} copy(f32[32,8,8,16]{3,2,1,0:T(8,128)} %bitcast.11) | data formatting | bytes 262144 | tf_op jit(solution)/shard_map/reshape | solution.py:421
  145.8 1.0 copy.27
  146.7 0.0 copy-done.16
  146.7 0.6 copy.26
  147.4 1.0 copy.28
  148.4 0.6 copy.30
Async XLA Ops:
  0.6 2.9 %copy-start.11 = (f32[16,128]{1,0:T(8,128)S(1)}, f32[16,128]{1,0:T(8,128)}, u32[]{:S(2)}) copy-start(f32[16,128]{1,0:T(8,128)} %decay_log.7) | copy-start | bytes 24580
  0.6 2.9 %copy-start.2 = (f32[32,64,128]{2,1,0:T(8,128)S(1)}, f32[32,64,128]{2,1,0:T(8,128)}, u32[]{:S(2)}) copy-start(f32[32,64,128]{2,1,0:T(8,128)} %feat.5) | copy-start | bytes 3145732
  2.0 46.8 %copy-start = (f32[32,64,16]{2,1,0:T(8,128)}, f32[32,64,16]{2,1,0:T(8,128)S(1)}, u32[]{:S(2)}) copy-start(f32[32,64,16]{2,1,0:T(8,128)S(1)} %copy.23.write) | copy-start | bytes 393220
  3.5 1.2 copy-start.3
  4.8 1.2 copy-start.4
  6.0 42.9 %copy-start.1 = (f32[32,64,16]{2,1,0:T(8,128)}, f32[32,64,16]{2,1,0:T(8,128)S(1)}, u32[]{:S(2)}) copy-start(f32[32,64,16]{2,1,0:T(8,128)S(1)} %copy.24.read) | copy-start | bytes 393220
  22.1 46.2 %copy-start.5 = (f32[32,16,8,128]{3,2,1,0:T(8,128)}, f32[32,16,8,128]{3,2,1,0:T(8,128)S(1)}, u32[]{:S(2)}) copy-start(f32[32,16,8,128]{3,2,1,0:T(8,128)S(1)} %get-tuple-element.32.later) | copy-start | bytes 6291460
  22.1 46.2 %copy-start.9 = (f32[32,8,128]{2,1,0:T(8,128)}, f32[32,8,128]{2,1,0:T(8,128)S(1)}, u32[]{:S(2)}) copy-start(f32[32,8,128]{2,1,0:T(8,128)S(1)} %get-tuple-element.31.before) | copy-start | bytes 393220
  22.1 46.2 %copy-start.14 = (f32[32,1,128]{2,1,0:T(1,128)}, f32[32,1,128]{2,1,0:T(1,128)S(1)}, u32[]{:S(2)}) copy-start(f32[32,1,128]{2,1,0:T(1,128)S(1)} %get-tuple-element.28.refs_3_.sum_cols) | copy-start | bytes 49156
  48.8 19.5 %copy-start.6 = (f32[8,16,8,128]{3,2,1,0:T(8,128)}, f32[8,16,8,128]{3,2,1,0:T(8,128)S(1)}, u32[]{:S(2)}) copy-start(f32[8,16,8,128]{3,2,1,0:T(8,128)S(1)} %get-tuple-element.29.from_above) | copy-start | bytes 1572868
  48.9 19.5 %copy-start.8 = (f32[32,16,128]{2,1,0:T(8,128)}, f32[32,16,128]{2,1,0:T(8,128)S(1)}, u32[]{:S(2)}) copy-start(f32[32,16,128]{2,1,0:T(8,128)S(1)} %get-tuple-element.30.from_right) | copy-start | bytes 786436
  68.4 1.3 copy-start.7
  89.4 0.8 copy-start.10
  90.2 0.7 copy-start.13
  90.9 41.7 %copy-start.12 = (f32[16,128]{1,0:T(8,128)S(1)}, f32[16,128]{1,0:T(8,128)}, u32[]{:S(2)}) copy-start(f32[16,128]{1,0:T(8,128)} %decay_log.7) | copy-start | bytes 24580
  132.6 0.8 copy-start.15
  133.5 13.3 %copy-start.16 = (f32[32,64,16]{2,1,0:T(8,128)S(1)}, f32[32,64,16]{2,1,0:T(8,128)}, u32[]{:S(2)}) copy-start(f32[32,64,16]{2,1,0:T(8,128)} %get-tuple-element.43) | copy-start | bytes 393220

commit v3 on v0

v3 whole, which is shorter than its diff:
```python
import functools
import math
import jax
import jax.numpy as jnp
from jax import lax
from jax.experimental import pallas as pl
from jax.experimental.pallas import tpu as pltpu
from jax.sharding import PartitionSpec as P

NS = 16
HALF = 8
D = 128
S = 8
BLOCK = 4
F32 = jnp.float32
BF16 = jnp.bfloat16
LOG2E = math.log2(math.e)
LN2 = math.log(2.0)
MESH = pl.DeviceIdType.MESH
VMEM = pl.BlockSpec(memory_space=pltpu.VMEM)


def column(ref, h, k, width):
    return ref[h, pl.ds(k, S, stride=width), :]


def set_rates(decay_log, rates):
    for n in range(NS):
        rates[n] = jnp.broadcast_to(-jnp.exp(decay_log[n : n + 1, :]) * LOG2E, (S, D))


def equal(a, b):
    return jnp.where(a == b, 1.0, 0.0).astype(BF16)


def set_spreader(spreader):
    of = lax.broadcasted_iota(jnp.int32, spreader.shape, 0) % NS
    to = lax.broadcasted_iota(jnp.int32, spreader.shape, 1) // D
    spreader[...] = equal(of, to)


def set_selector(selector):
    of = lax.broadcasted_iota(jnp.int32, selector.shape, 0) // D
    to = lax.broadcasted_iota(jnp.int32, selector.shape, 1)
    selector[...] = equal(of, to)


def by_segment(cols):
    K = cols // S
    at = lax.broadcasted_iota(jnp.int32, (cols, cols), 0)
    col = lax.broadcasted_iota(jnp.int32, (cols, cols), 1)
    return equal(col, (at % S) * K + at // S)


def split3(x, axis):
    high = x.astype(BF16)
    rest = x - high.astype(F32)
    mid = rest.astype(BF16)
    low = (rest - mid.astype(F32)).astype(BF16)
    return jnp.concatenate([high, mid, low], axis=axis)


def spread(coded, spreader, pair):
    return jnp.dot(coded, spreader[:, 2 * D * pair : 2 * D * pair + 2 * D],
                   preferred_element_type=F32)


def sublane():
    return lax.broadcasted_iota(jnp.int32, (S, D), 0)


def sums_down(value, at):
    for shift in (1, 2, 4):
        value = value + jnp.where(at >= shift, pltpu.roll(value, shift, 0), 0.0)
    return value


def sums_up(value, at):
    for shift in (1, 2, 4):
        value = value + jnp.where(at < S - shift, pltpu.roll(value, S - shift, 0), 0.0)
    return value


def tile_of(block, row, half):
    return block[row : row + S, D * half : D * half + D]


def carries_kernel(nr, nc, feat, step, write, read, grad, decay_log,
                   from_above, from_right, from_left, from_below,
                   sum_cols, before, later, earlier, coded,
                   rates, spreader, drive, vert, leave_v, leave_a, leave_p, leave_s, sum_rows,
                   sums_r, sums_c, in_r, in_c, out_r, out_c,
                   s_out, s_in, b_out, b_in, q_out, q_in):
    rows, cols = step.shape[0], step.shape[1]
    K = cols // S
    ri, ci = lax.axis_index("row"), lax.axis_index("col")
    kr, hc = K // nr, rows // nc
    row_peers = [(lax.rem(ri + o, nr), ci) for o in range(1, nr)]
    col_peers = [(ri, lax.rem(ci + o, nc)) for o in range(1, nc)]
    barrier = pltpu.get_barrier_semaphore()
    for peer in row_peers + col_peers:
        pl.semaphore_signal(barrier, inc=1, device_id=peer, device_id_type=MESH)

    set_rates(decay_log, rates)
    set_spreader(spreader)
    slow = -jnp.exp(decay_log[...]) * LOG2E
    at = sublane()
    turn = by_segment(cols)

    def code(h, carry):
        for i, ref in enumerate((write, read)):
            parts = split3(ref[h], 0)
            coded[h, cols * i : cols * i + cols, :] = lax.dot_general(
                turn, parts, (((1,), (1,)), ((), ())), preferred_element_type=F32).astype(BF16)
        return carry

    lax.fori_loop(0, rows, code, 0, unroll=4)
    leave_v[...] = jnp.zeros_like(leave_v)
    leave_p[...] = jnp.zeros_like(leave_p)
    sum_rows[...] = jnp.zeros_like(sum_rows)

    def local_leaves(half):
        def row(h, carry):
            total = jnp.zeros((S, D), F32)
            for k in range(K):
                dt = column(step, h, k, K)
                drive[k] = dt * column(feat, h, k, K)
                if half == 0:
                    total = total + dt
                    sum_rows[k] += dt
            if half == 0:
                upto = sums_down(total, at)
                before[h] = upto - total
                sum_cols[h] = upto[S - 1 :, :]
            ahead = before[h]
            both = coded[h]
            for pair in range(HALF // 2):
                spreads = spread(both, spreader, half * HALF // 2 + pair)
                for j in range(2):
                    i = 2 * pair + j
                    n = half * HALF + i
                    a = jnp.zeros((S, D), F32)
                    r2 = rates[n]
                    for k in reversed(range(K)):
                        e = jnp.exp2(column(step, h, k, K) * r2)
                        leave_v[half, k, i] = (
                            e * leave_v[half, k, i] + drive[k] * tile_of(spreads, S * k, j))
                        a = e * (a + tile_of(spreads, cols + S * k, j) * column(grad, h, k, K))
                    m = jnp.exp2(r2 * ahead) * a
                    z = sums_up(m, at)
                    leave_a[half, h, i : i + 1, :] = z[0:1, :]
                    later[h, n] = z - m
            return carry

        lax.fori_loop(0, rows, row, 0)

    def carried_leaves(half):
        vert[half] = from_above[half]

        def row(step_at, carry):
            h = step_at
            b = rows - 1 - step_at
            total_h = jnp.zeros((S, D), F32)
            total_b = jnp.zeros((S, D), F32)
            for k in range(K):
                dt = column(step, h, k, K)
                drive[k] = dt * column(feat, h, k, K)
                total_h = total_h + dt
                total_b = total_b + column(step, b, k, K)
            upto_h = before[h] + total_h
            upto_b = before[b] + total_b
            rate = slow[half * HALF : half * HALF + HALF]
            whole = jnp.exp2(rate * sum_cols[h])
            entering = jnp.exp2(rate * sum_cols[b]) * from_right[half, b]
            both = jnp.concatenate([coded[h, :cols, :], coded[b, cols:, :]], axis=0)
            for pair in range(HALF // 2):
                spreads = spread(both, spreader, half * HALF // 2 + pair)
                for j in range(2):
                    i = 2 * pair + j
                    n = half * HALF + i
                    r2 = rates[n]
                    l = jnp.zeros((S, D), F32)
                    for k in range(K):
                        e = jnp.exp2(column(step, h, k, K) * r2)
                        v = e * vert[half, k, i] + drive[k] * tile_of(spreads, S * k, j)
                        vert[half, k, i] = v
                        l = e * l + v
                    m = jnp.exp2(-r2 * upto_h) * l
                    z = sums_down(m, at)
                    leave_s[half, h, i : i + 1, :] = whole[i : i + 1, :] * z[S - 1 :, :]
                    earlier[h, n] = z - m
                    a = jnp.exp2(-r2 * upto_b) * (later[b, n] + entering[i : i + 1, :])
                    for k in reversed(range(K)):
                        e = jnp.exp2(column(step, b, k, K) * r2)
                        ah = a + tile_of(spreads, cols + S * k, j) * column(grad, b, k, K)
                        leave_p[half, k, i] = e * (ah + leave_p[half, k, i])
                        a = e * ah
            return carry

        lax.fori_loop(0, rows, row, 0)

    def send(src, dst, out_sem, in_sem, peer):
        copy = pltpu.make_async_remote_copy(
            src_ref=src, dst_ref=dst, send_sem=out_sem, recv_sem=in_sem,
            device_id=peer, device_id_type=MESH)
        copy.start()
        return copy

    def scatter(x, half, leave_r, leave_c):
        copies = []
        for o, peer in enumerate(row_peers):
            copies.append(send(leave_r.at[half, pl.ds(peer[0] * kr, kr)], in_r.at[x, half, ri],
                               s_out.at[x, half, o], s_in.at[x, half, o], peer))
            if x == 0 and half == 0:
                copies.append(send(sum_rows.at[pl.ds(peer[0] * kr, kr)], sums_r.at[ri],
                                   q_out.at[o], q_in.at[o], peer))
        for p, peer in enumerate(col_peers):
            o = nr - 1 + p
            copies.append(send(leave_c.at[half, pl.ds(peer[1] * hc, hc)], in_c.at[x, half, ci],
                               s_out.at[x, half, o], s_in.at[x, half, o], peer))
            if x == 0 and half == 0:
                copies.append(send(sum_cols.at[pl.ds(peer[1] * hc, hc)], sums_c.at[ci],
                                   q_out.at[o], q_in.at[o], peer))
        in_r[x, half, ri] = leave_r[half, pl.ds(ri * kr, kr)]
        in_c[x, half, ci] = leave_c[half, pl.ds(ci * hc, hc)]
        if x == 0 and half == 0:
            sums_r[ri] = sum_rows[pl.ds(ri * kr, kr)]
            sums_c[ci] = sum_cols[pl.ds(ci * hc, hc)]
        return copies

    def give_back(x, half, waiting, got_r, got_c):
        for copy in waiting:
            copy.wait()
        rate = slow[half * HALF : half * HALF + HALF]
        for j in range(hc):
            now = jnp.zeros((HALF, D), F32)
            for c in (reversed(range(nc)) if x == 0 else range(nc)):
                out_c[x, half, c, j] = now
                now = jnp.exp2(rate * sums_c[c, j]) * now + in_c[x, half, c, j]

        def scan_row(i, carry):
            r2 = rates[half * HALF + i]
            for j in range(kr):
                now = jnp.zeros((S, D), F32)
                for r in (range(nr) if x == 0 else reversed(range(nr))):
                    out_r[x, half, r, j, i] = now
                    now = jnp.exp2(r2 * sums_r[r, j]) * now + in_r[x, half, r, j, i]
            return carry

        lax.fori_loop(0, HALF, scan_row, 0)
        copies = []
        for o, peer in enumerate(row_peers):
            copies.append(send(out_r.at[x, half, peer[0]], got_r.at[half, pl.ds(ri * kr, kr)],
                               b_out.at[x, half, o], b_in.at[x, half, o], peer))
        for p, peer in enumerate(col_peers):
            o = nr - 1 + p
            copies.append(send(out_c.at[x, half, peer[1]], got_c.at[half, pl.ds(ci * hc, hc)],
                               b_out.at[x, half, o], b_in.at[x, half, o], peer))
        got_r[half, pl.ds(ri * kr, kr)] = out_r[x, half, ri]
        got_c[half, pl.ds(ci * hc, hc)] = out_c[x, half, ci]
        return copies

    def arrive(copies):
        for copy in copies:
            copy.wait()

    local_leaves(0)
    pl.semaphore_wait(barrier, len(row_peers) + len(col_peers))
    one = scatter(0, 0, leave_v, leave_a)
    local_leaves(1)
    two = scatter(0, 1, leave_v, leave_a)
    one = give_back(0, 0, one, from_above, from_right)
    two = give_back(0, 1, two, from_above, from_right)
    arrive(one)
    carried_leaves(0)
    one = scatter(1, 0, leave_p, leave_s)
    arrive(two)
    carried_leaves(1)
    two = scatter(1, 1, leave_p, leave_s)
    one = give_back(1, 0, one, from_below, from_left)
    two = give_back(1, 1, two, from_below, from_left)
    arrive(one)
    arrive(two)


def channel_sums(products, selector, turn, out, base, cols):
    values = products[...]
    high = values.astype(BF16)
    low = (values - high.astype(F32)).astype(BF16)
    sums = jnp.dot(high, selector[...], preferred_element_type=F32)
    sums = sums + jnp.dot(low, selector[...], preferred_element_type=F32)
    for b in range(BLOCK):
        parts = split3(sums[b * cols : b * cols + cols, :NS], 1)
        turned = lax.dot_general(parts, turn, (((0,), (0,)), ((), ())),
                                 preferred_element_type=F32)
        out[base + b] = turned[:NS] + turned[NS : 2 * NS] + turned[2 * NS :]


def outputs_kernel(feat, step, grad, decay_log, from_above, from_right, from_left, from_below,
                   sum_cols, before, later, earlier, coded,
                   g_feat, g_step, g_write, g_read, g_decay,
                   rates, spreader, selector, drive, vert, below, kept_s, kept_v, products):
    rows, cols = step.shape[0], step.shape[1]
    K = cols // S
    set_rates(decay_log, rates)
    set_spreader(spreader)
    set_selector(selector)
    turn = by_segment(cols)
    vert[...] = from_above[...]
    below[...] = from_below[...]
    g_decay[...] = jnp.zeros_like(g_decay)
    slow = -jnp.exp(decay_log[...]) * LOG2E

    def forward(base, within, carry):
        h = base + within
        for k in range(K):
            drive[k] = column(step, h, k, K) * column(feat, h, k, K)
        ahead = before[h]
        only = coded[h, :cols, :]
        for pair in range(NS // 2):
            spreads = spread(only, spreader, pair)
            for j in range(2):
                n = 2 * pair + j
                half, i = divmod(n, HALF)
                r2 = rates[n]
                s = jnp.exp2(r2 * ahead) * (earlier[h, n] + from_left[half, h, i : i + 1, :])
                for k in range(K):
                    e = jnp.exp2(column(step, h, k, K) * r2)
                    q = e * vert[half, k, i]
                    v = q + drive[k] * tile_of(spreads, S * k, j)
                    vert[half, k, i] = v
                    t = e * s
                    s = t + v
                    kept_v[h, k, n] = q
                    kept_s[h, k, n] = t
                    products[pl.ds(cols * within + S * k, S), D * n : D * n + D] = (
                        s * column(grad, h, k, K))
        return carry

    def backward(base, back, carry):
        within = BLOCK - 1 - back
        h = base + within
        total = jnp.zeros((S, D), F32)
        for k in range(K):
            dt = column(step, h, k, K)
            drive[k] = dt * column(feat, h, k, K)
            total = total + dt
        upto = before[h] + total
        gone = jnp.exp2(slow * sum_cols[h])
        both = coded[h]
        through = [jnp.zeros((S, D), F32)] * K
        rated = [jnp.zeros((S, D), F32)] * K
        for pair in range(NS // 2):
            spreads = spread(both, spreader, pair)
            for j in range(2):
                n = 2 * pair + j
                half, i = divmod(n, HALF)
                r2 = rates[n]
                entering = gone[n : n + 1, :] * from_right[half, h, i : i + 1, :]
                a = jnp.exp2(-r2 * upto) * (later[h, n] + entering)
                stepped = jnp.zeros((S, D), F32)
                for k in reversed(range(K)):
                    dt = column(step, h, k, K)
                    e = jnp.exp2(dt * r2)
                    ah = a + tile_of(spreads, cols + S * k, j) * column(grad, h, k, K)
                    av = ah + below[half, k, i]
                    below[half, k, i] = e * av
                    a = e * ah
                    eg = ah * kept_s[h, k, n] + av * kept_v[h, k, n]
                    through[k] = through[k] + av * tile_of(spreads, S * k, j)
                    rated[k] = rated[k] + eg * r2
                    stepped = stepped + eg * dt
                    products[pl.ds(cols * within + S * k, S), D * n : D * n + D] = av * drive[k]
                g_decay[n] += stepped
        for k in range(K):
            g_feat[h, pl.ds(k, S, stride=K), :] = column(step, h, k, K) * through[k]
            g_step[h, pl.ds(k, S, stride=K), :] = (
                column(feat, h, k, K) * through[k] + LN2 * rated[k])
        return carry

    def forward_block(b, carry):
        lax.fori_loop(0, BLOCK, functools.partial(forward, b * BLOCK), 0)
        channel_sums(products, selector, turn, g_read, b * BLOCK, cols)
        return carry

    def backward_block(b, carry):
        base = rows - BLOCK - b * BLOCK
        lax.fori_loop(0, BLOCK, functools.partial(backward, base), 0)
        channel_sums(products, selector, turn, g_write, base, cols)
        return carry

    lax.fori_loop(0, rows // BLOCK, forward_block, 0)
    lax.fori_loop(0, rows // BLOCK, backward_block, 0)


def total_kernel(nr, nc, part, decay_log, out, by_row, by_col, s_out, s_in):
    ri, ci = lax.axis_index("row"), lax.axis_index("col")
    row_peers = [(lax.rem(ri + o, nr), ci) for o in range(1, nr)]
    col_peers = [(ri, lax.rem(ci + o, nc)) for o in range(1, nc)]
    barrier = pltpu.get_barrier_semaphore()
    for peer in row_peers + col_peers:
        pl.semaphore_signal(barrier, inc=1, device_id=peer, device_id_type=MESH)
    pl.semaphore_wait(barrier, len(row_peers) + len(col_peers))

    def stage(value, box, mine, peers, base):
        box[mine] = value
        copies = []
        for o, peer in enumerate(peers):
            copy = pltpu.make_async_remote_copy(
                src_ref=box.at[mine], dst_ref=box.at[mine], send_sem=s_out.at[base + o],
                recv_sem=s_in.at[base + o], device_id=peer, device_id_type=MESH)
            copy.start()
            copies.append(copy)
        for copy in copies:
            copy.wait()
        return jnp.sum(box[...], axis=0)

    value = stage(jnp.sum(part[...], axis=1), by_row, ri, row_peers, 0)
    value = stage(value, by_col, ci, col_peers, nr - 1)
    out[...] = value * -jnp.exp(decay_log[...])


def total(nr, nc, part, decay_log):
    dma = pltpu.SemaphoreType.DMA((nr + nc - 2,))
    return pl.pallas_call(
        functools.partial(total_kernel, nr, nc),
        out_shape=jax.ShapeDtypeStruct((NS, D), F32),
        in_specs=[VMEM] * 2,
        out_specs=VMEM,
        scratch_shapes=[pltpu.VMEM((nr, NS, D), F32), pltpu.VMEM((nc, NS, D), F32), dma, dma],
        compiler_params=pltpu.CompilerParams(
            collective_id=1, has_side_effects=True, vmem_limit_bytes=4 << 20),
        name="total",
    )(part, decay_log)


def shards(features, step_size, write_weights, read_weights, decay_log, out_grad):
    rows, cols = step_size.shape[0], step_size.shape[1]
    K = cols // S
    nr, nc = lax.axis_size("row"), lax.axis_size("col")
    kr, hc, peers = K // nr, rows // nc, nr + nc - 2
    sds = jax.ShapeDtypeStruct
    vm = pltpu.VMEM
    carry_r, carry_c = (2, K, HALF, S, D), (2, rows, HALF, D)
    rates, spreader = vm((NS, S, D), F32), vm((3 * NS, NS * D), BF16)
    drive = vm((K, S, D), F32)
    write_t, read_t = write_weights.transpose(0, 2, 1), read_weights.transpose(0, 2, 1)

    outs = [carry_r, carry_c, carry_c, carry_r, (rows, 1, D), (rows, S, D),
            (rows, NS, S, D), (rows, NS, S, D)]
    outs = [sds(o, F32) for o in outs] + [sds((rows, 2 * cols, 3 * NS), BF16)]
    args = (features, step_size, write_t, read_t, out_grad, decay_log)
    box_r, box_c = vm((2, 2, nr, kr, HALF, S, D), F32), vm((2, 2, nc, hc, HALF, D), F32)
    dma = pltpu.SemaphoreType.DMA((2, 2, peers))
    few = pltpu.SemaphoreType.DMA((peers,))
    passed = pl.pallas_call(
        functools.partial(carries_kernel, nr, nc),
        out_shape=outs,
        in_specs=[VMEM] * len(args),
        out_specs=[VMEM] * len(outs),
        scratch_shapes=[
            rates, spreader, drive, vm(carry_r, F32), vm(carry_r, F32), vm(carry_c, F32),
            vm(carry_r, F32), vm(carry_c, F32), vm((K, S, D), F32),
            vm((nr, kr, S, D), F32), vm((nc, hc, 1, D), F32),
            box_r, box_c, box_r, box_c, dma, dma, dma, dma, few, few],
        compiler_params=pltpu.CompilerParams(
            collective_id=0, has_side_effects=True, vmem_limit_bytes=30 << 20),
        name="carries",
    )(*args)

    args = (features, step_size, out_grad, decay_log) + tuple(passed)
    outs = [(rows, cols, D), (rows, cols, D), (rows, NS, cols), (rows, NS, cols), (NS, S, D)]
    g_feat, g_step, g_write, g_read, g_decay = pl.pallas_call(
        outputs_kernel,
        out_shape=[sds(o, F32) for o in outs],
        in_specs=[VMEM] * len(args),
        out_specs=[VMEM] * len(outs),
        scratch_shapes=[
            rates, spreader, vm((NS * D, D), BF16), drive, vm(carry_r, F32), vm(carry_r, F32),
            vm((rows, K, NS, S, D), F32), vm((rows, K, NS, S, D), F32),
            vm((BLOCK * cols, NS * D), F32)],
        compiler_params=pltpu.CompilerParams(vmem_limit_bytes=60 << 20),
        name="outputs",
    )(*args)
    g_decay = total(nr, nc, g_decay, decay_log)
    return (g_feat, g_step, g_write.transpose(0, 2, 1), g_read.transpose(0, 2, 1), g_decay)


def solution(mesh):
    tiles = P("row", "col", None)
    in_specs = (tiles, tiles, tiles, tiles, P(), tiles)
    out_specs = (tiles, tiles, tiles, tiles, P())
    return jax.shard_map(shards, mesh=mesh, in_specs=in_specs, out_specs=out_specs, check_vma=False)
```

time: 984 us -> 138 us (0.14); the launches traced: 968 us -> 138 us
  other arithmetic: 690 us -> 0 us
  Pallas kernels: 0 us -> 121 us
  local copies, waits for them, and re-layouts: 98.4 us -> 15.6 us
  matrix products: 74.7 us -> 0 us
  blocking collectives: 64.6 us -> 0 us
  waiting for transfers between devices: 23 us -> 0 us
  between operations: 14.6 us -> 0.69 us
    dynamic_update_slice x192 -> x0, other arithmetic: 376 us -> none  [the longest x64 143 us: sweep_rows(): closing, values = lax.scan(advance, initial, (decays, driving))]
    mul x100 -> x0, other arithmetic: 147 us -> none  [the longest x64 76.4 us: advance(): current = factor * value]
    pallas_call x0 -> x3, Pallas kernels: none -> 121 us  [the longest x1 62.4 us: shards(): pl.pallas_call(functools.partial(carries_kernel, nr, nc), out_shape=outs,...]
    select_n x48 -> x0, other arithmetic: 76.4 us -> none  [lap(): return jax.tree.map(lambda a, b: jnp.where(reached, a, b), new, before)]
    dot_general x3 -> x0, matrix products: 74.7 us -> none  [the longest x1 28.9 us: shards(): jnp.einsum('hwnd,hwd->hwn', adjoint_v, step_size * features, precision=hi...]
    psum x1 -> x0, blocking collectives: 64.6 us -> none  [shards(): grad_decay = lax.psum(partial_sum, ('row', 'col')) * decay_rate]
    add x2 -> x0, other arithmetic: 35.4 us -> none  [the longest x1 23.2 us: shards(): local_cols + jnp.exp(running_cols[:, :, None, :] * decay_rate) * from_lef...]
    dot_general x1 -> x0, other arithmetic: 34.8 us -> none  [shards(): jnp.einsum('hwnd,hwd->nd', exponent_grad, step_size, precision=highest)]
  transfers between devices with their start and end apart: 6 -> 0, of which waited for: 1 -> 0; matrix products, arithmetic and copies ran while one was open for 48% -> 0% of each run, Pallas kernels for 0% -> 0%
where the time goes in v3:
time: 138 us
  Pallas kernels  121 us (88%)
  local copies, waits for them, and re-layouts  15.6 us (11%)
    pallas_call x1, Pallas kernels, shards(): pl.pallas_call(functools.partial(carries_kernel, nr, nc), out_shape=outs,...  62.4 us
    pallas_call x1, Pallas kernels, shards(): pl.pallas_call(outputs_kernel, out_shape=[sds(o, F32) for o in outs], in_...  47.1 us
    unnamed x35, local copies, waits for them, and re-layouts  15.6 us
    pallas_call x1, Pallas kernels, total(): pl.pallas_call(functools.partial(total_kernel, nr, nc), out_shape=jax.Sha...  12 us

profile of v3, /device:TPU:1, one launch (start us, length us, event | category | flops | bytes accessed | tf_op | source)
XLA Modules:
  0.0 137.8 jit_solution(2573614184130123402)
XLA Ops:
  0.6 0.0 copy-start
  0.6 1.2 copy-done
  1.9 0.0 copy-start.1
  1.9 1.2 copy-done.1
  3.1 0.0 copy-start.2
  3.1 1.2 copy-done.2
  4.3 0.0 copy-start.8
  4.3 0.9 copy-done.8
  5.3 0.0 copy-start.9
  5.3 0.9 copy-done.9
  6.2 0.0 copy-start.13
  6.2 0.7 copy-done.13
  6.9 62.4 %carries.1 = (f32[2,8,8,8,128]{4,3,2,1,0:T(8,128)S(1)}, f32[2,32,8,128]{3,2,1,0:T(8,128)S(1)}, f32[2,32,8,128]{3,2,1,0:T(8,128)S(1)}, f32[2,8,8,8,128]{4,3,2,1,0...) custom-call(f32[32,64,128]{2,1,0:T(8,128)S(1)} %copy-done, ...), custom_call_target="tpu_custom_call" | custom-call | tf_op jit(solution)/shard_map/carries/pallas_call | solution.py:456
  69.3 0.0 copy-start.3
  69.3 1.3 copy-done.3
  70.6 0.0 copy-start.4
  70.6 1.3 copy-done.4
  72.0 0.0 copy-start.5
  72.0 1.0 copy-done.5
  72.9 0.0 copy-start.6
  72.9 0.8 copy-done.6
  73.8 0.0 copy-start.7
  73.8 0.8 copy-done.7
  74.6 0.0 copy-start.10
  74.6 0.7 copy-done.10
  75.3 0.0 copy-start.11
  75.3 0.7 copy-done.11
  76.0 0.0 copy-start.12
  76.0 0.6 copy-done.12
  76.7 0.0 copy-start.16
  76.7 0.6 copy-done.16
  77.3 0.0 copy-start.14
  77.3 47.1 %outputs.1 = (f32[32,64,128]{2,1,0:T(8,128)}, f32[32,64,128]{2,1,0:T(8,128)}, f32[32,16,64]{2,1,0:T(8,128)}, f32[32,16,64]{2,1,0:T(8,128)}, f32[16,8,128]{2,1,0:T(8,128)}) custom-call(f32[32,64,128]{2,1,0:T(8,128)} %feat.3, f32[32,64,128]{2,1,0:T(8,128)} %step.3, f32[32,64,128]{2,1,0:T(8,128)} %grad.3, f32[16,128]{1,0:T(8,128)} %decay_log.5, ...), custom_call_target="tpu_custom_call" | custom-call | tf_op jit(solution)/shard_map/outputs/pallas_call | solution.py:473
  124.4 0.0 copy-done.14
  124.4 0.0 copy-start.15
  124.4 0.8 copy-done.15
  125.2 12.0 %total.1 = f32[16,128]{1,0:T(8,128)S(1)} custom-call(f32[16,8,128]{2,1,0:T(8,128)S(1)} %copy-done.15, f32[16,128]{1,0:T(8,128)S(1)} %copy-done.14), custom_call_target="tpu_custom_call" | custom-call | tf_op jit(solution)/shard_map/total/pallas_call | solution.py:425
  137.2 0.6 copy.12
Async XLA Ops:
  0.6 1.2 copy-start
  1.9 1.2 copy-start.1
  3.1 1.2 copy-start.2
  4.3 0.9 copy-start.8
  5.3 0.9 copy-start.9
  6.2 0.7 copy-start.13
  69.3 1.3 copy-start.3
  70.6 1.3 copy-start.4
  72.0 1.0 copy-start.5
  72.9 0.8 copy-start.6
  73.8 0.8 copy-start.7
  74.6 0.7 copy-start.10
  75.3 0.7 copy-start.11
  76.0 0.6 copy-start.12
  76.7 0.6 copy-start.16
  77.3 47.1 %copy-start.14 = (f32[16,128]{1,0:T(8,128)S(1)}, f32[16,128]{1,0:T(8,128)}, u32[]{:S(2)}) copy-start(f32[16,128]{1,0:T(8,128)} %decay_log.5) | copy-start | bytes 24580
  124.4 0.8 copy-start.15

commit v4 on v0

v4 whole, which is shorter than its diff:
```python
import functools
import math
import jax
import jax.numpy as jnp
from jax import lax
from jax.experimental import pallas as pl
from jax.experimental.pallas import tpu as pltpu
from jax.sharding import PartitionSpec as P

NS = 16
HALF = 8
D = 128
S = 8
F32 = jnp.float32
BF16 = jnp.bfloat16
LOG2E = math.log2(math.e)
LN2 = math.log(2.0)
MESH = pl.DeviceIdType.MESH
VMEM = pl.BlockSpec(memory_space=pltpu.VMEM)


def column(ref, h, k, width):
    return ref[h, pl.ds(k, S, stride=width), :]


def set_rates(decay_log, rates):
    for n in range(NS):
        rates[n] = jnp.broadcast_to(-jnp.exp(decay_log[n : n + 1, :]) * LOG2E, (S, D))


def equal(a, b):
    return jnp.where(a == b, 1.0, 0.0).astype(BF16)


def set_spreader(spreader):
    of = lax.broadcasted_iota(jnp.int32, spreader.shape, 0) % NS
    to = lax.broadcasted_iota(jnp.int32, spreader.shape, 1) // D
    spreader[...] = equal(of, to)


def by_segment(cols):
    K = cols // S
    at = lax.broadcasted_iota(jnp.int32, (cols, cols), 0)
    col = lax.broadcasted_iota(jnp.int32, (cols, cols), 1)
    return equal(col, (at % S) * K + at // S)


def split3(x, axis):
    high = x.astype(BF16)
    rest = x - high.astype(F32)
    mid = rest.astype(BF16)
    low = (rest - mid.astype(F32)).astype(BF16)
    return jnp.concatenate([high, mid, low], axis=axis)


def spread(coded, spreader, pair):
    return jnp.dot(coded, spreader[:, 2 * D * pair : 2 * D * pair + 2 * D],
                   preferred_element_type=F32)


def sublane():
    return lax.broadcasted_iota(jnp.int32, (S, D), 0)


def sums_down(value, at):
    for shift in (1, 2, 4):
        value = value + jnp.where(at >= shift, pltpu.roll(value, shift, 0), 0.0)
    return value


def tile_of(block, row, half):
    return block[row : row + S, D * half : D * half + D]


def states_of(half):
    return slice(half * HALF, half * HALF + HALF)


def add_sums(total, products, picker, n):
    values = products[n]
    high = values.astype(BF16)
    low = (values - high.astype(F32)).astype(BF16)
    return total + lax.dot_general(
        picker[n], jnp.concatenate([high, low], axis=1), (((1,), (1,)), ((), ())),
        preferred_element_type=F32)


def scan_kernel(nr, nc, feat, step, write, read, grad, decay_log,
                g_feat, g_step, g_write, g_read, g_decay,
                rates, slow, spreader, picker, coded, steps, grads, drive,
                before, upto, sum_cols, sum_rows, later, earlier, mix,
                leave_v, leave_p, vert, from_above, from_below,
                leave_a, leave_s, from_right, from_left, kept_s, kept_v, even, odd, part,
                sums_r, sums_c, in_v, out_v, in_p, out_p, in_a, out_a, in_s, out_s,
                by_row, by_col, row_sems, col_sems):
    rows, cols = step.shape[0], step.shape[1]
    K = cols // S
    ri, ci = lax.axis_index("row"), lax.axis_index("col")
    kr, hc = K // nr, rows // nc
    row_peers = [(lax.rem(ri + o, nr), ci) for o in range(1, nr)]
    col_peers = [(ri, lax.rem(ci + o, nc)) for o in range(1, nc)]
    barrier = pltpu.get_barrier_semaphore()
    for peer in row_peers + col_peers:
        pl.semaphore_signal(barrier, inc=1, device_id=peer, device_id_type=MESH)

    set_rates(decay_log, rates)
    set_spreader(spreader)
    slow[...] = -jnp.exp(decay_log[...]) * LOG2E
    picked = lax.broadcasted_iota(jnp.int32, picker.shape[1:], 0)
    for n in range(NS):
        picker[n] = equal(picked, n)
    leave_v[...] = jnp.zeros_like(leave_v)
    leave_p[...] = jnp.zeros_like(leave_p)
    sum_rows[...] = jnp.zeros_like(sum_rows)
    part[...] = jnp.zeros_like(part)
    at = sublane()
    turn = by_segment(cols)

    def code(h, carry):
        for i, ref in enumerate((write, read)):
            parts = split3(ref[h], 0)
            coded[h, cols * i : cols * i + cols, :] = lax.dot_general(
                turn, parts, (((1,), (1,)), ((), ())), preferred_element_type=F32).astype(BF16)
        return carry

    def over(lo, hi, row):
        def one(i, carry):
            row(i)
            return carry

        lax.fori_loop(lo, hi, one, 0)

    def local_vertical(half, h):
        if half == 0:
            total = jnp.zeros((S, D), F32)
            for k in range(K):
                dt = column(step, h, k, K)
                steps[h, k] = dt
                drive[h, k] = dt * column(feat, h, k, K)
                total = total + dt
                sum_rows[k] += dt
            ends = sums_down(total, at)
            upto[h] = ends
            before[h] = ends - total
            sum_cols[h] = ends[S - 1 :, :]
        only = coded[h, :cols, :]
        for pair in range(HALF // 2):
            spreads = spread(only, spreader, half * HALF // 2 + pair)
            for j in range(2):
                i = 2 * pair + j
                r2 = rates[half * HALF + i]
                for k in range(K):
                    e = jnp.exp2(steps[h, k] * r2)
                    leave_v[half, k, i] = (
                        e * leave_v[half, k, i] + drive[h, k] * tile_of(spreads, S * k, j))

    def local_adjoint(h):
        for k in range(K):
            grads[h, k] = column(grad, h, k, K)
        only = coded[h, cols:, :]
        ahead = before[h]
        for pair in range(NS // 2):
            spreads = spread(only, spreader, pair)
            for j in range(2):
                n = 2 * pair + j
                r2 = rates[n]
                a = jnp.zeros((S, D), F32)
                for k in reversed(range(K)):
                    e = jnp.exp2(steps[h, k] * r2)
                    a = e * (a + tile_of(spreads, S * k, j) * grads[h, k])
                mix[S * n : S * n + S, :] = jnp.exp2(r2 * ahead) * a
        for half in range(2):
            passed = jnp.zeros((HALF, D), F32)
            for g in reversed(range(S)):
                later[h, half, HALF * g : HALF * g + HALF, :] = passed
                passed = passed + mix[pl.ds(S * HALF * half + g, HALF, stride=S), :]
            leave_a[h, half] = passed

    def carried_states(h):
        only = coded[h, :cols, :]
        ends = upto[h]
        for pair in range(NS // 2):
            spreads = spread(only, spreader, pair)
            for j in range(2):
                n = 2 * pair + j
                half, i = divmod(n, HALF)
                r2 = rates[n]
                l = jnp.zeros((S, D), F32)
                for k in range(K):
                    e = jnp.exp2(steps[h, k] * r2)
                    v = e * vert[half, k, i] + drive[h, k] * tile_of(spreads, S * k, j)
                    vert[half, k, i] = v
                    l = e * l + v
                mix[S * n : S * n + S, :] = jnp.exp2(-r2 * ends) * l
        for half in range(2):
            passed = jnp.zeros((HALF, D), F32)
            for g in range(S):
                earlier[h, half, HALF * g : HALF * g + HALF, :] = passed
                passed = passed + mix[pl.ds(S * HALF * half + g, HALF, stride=S), :]
            leave_s[h, half] = jnp.exp2(slow[states_of(half), :] * sum_cols[h]) * passed

    def carried_adjoint(i):
        h = rows - 1 - i
        only = coded[h, cols:, :]
        ends = upto[h]
        for half in range(2):
            entering = jnp.exp2(slow[states_of(half), :] * sum_cols[h]) * from_right[h, half]
            for g in range(S):
                at_g = slice(HALF * g, HALF * g + HALF)
                later[h, half, at_g, :] = later[h, half, at_g, :] + entering
        for pair in range(NS // 2):
            spreads = spread(only, spreader, pair)
            for j in range(2):
                n = 2 * pair + j
                half, i = divmod(n, HALF)
                r2 = rates[n]
                a = jnp.exp2(-r2 * ends) * later[h, half, pl.ds(i, S, stride=HALF), :]
                for k in reversed(range(K)):
                    e = jnp.exp2(steps[h, k] * r2)
                    ah = a + tile_of(spreads, S * k, j) * grads[h, k]
                    leave_p[half, k, i] = e * (ah + leave_p[half, k, i])
                    a = e * ah

    def final_states(h, now, last):
        ahead = before[h]
        only = coded[h, :cols, :]
        for half in range(2):
            entering = from_left[h, half]
            for g in range(S):
                at_g = slice(HALF * g, HALF * g + HALF)
                earlier[h, half, at_g, :] = earlier[h, half, at_g, :] + entering
        sums = jnp.zeros((NS, cols), F32)
        for pair in range(NS // 2):
            spreads = spread(only, spreader, pair)
            for j in range(2):
                n = 2 * pair + j
                half, i = divmod(n, HALF)
                r2 = rates[n]
                s = jnp.exp2(r2 * ahead) * earlier[h, half, pl.ds(i, S, stride=HALF), :]
                for k in range(K):
                    e = jnp.exp2(steps[h, k] * r2)
                    q = e * from_above[half, k, i]
                    v = q + drive[h, k] * tile_of(spreads, S * k, j)
                    from_above[half, k, i] = v
                    t = e * s
                    s = t + v
                    kept_v[h, k, n] = q
                    kept_s[h, k, n] = t
                    now[n, pl.ds(k, S, stride=K), :] = s * grads[h, k]
                sums = add_sums(sums, last, picker, n)
        g_read[jnp.maximum(h - 1, 0)] = sums

    def final_adjoint(h, now, last):
        ends = upto[h]
        both = coded[h]
        through = [jnp.zeros((S, D), F32)] * K
        rated = [jnp.zeros((S, D), F32)] * K
        sums = jnp.zeros((NS, cols), F32)
        for pair in range(NS // 2):
            spreads = spread(both, spreader, pair)
            for j in range(2):
                n = 2 * pair + j
                half, i = divmod(n, HALF)
                r2 = rates[n]
                a = jnp.exp2(-r2 * ends) * later[h, half, pl.ds(i, S, stride=HALF), :]
                stepped = jnp.zeros((S, D), F32)
                for k in reversed(range(K)):
                    dt = steps[h, k]
                    e = jnp.exp2(dt * r2)
                    ah = a + tile_of(spreads, cols + S * k, j) * grads[h, k]
                    av = ah + from_below[half, k, i]
                    from_below[half, k, i] = e * av
                    a = e * ah
                    eg = ah * kept_s[h, k, n] + av * kept_v[h, k, n]
                    through[k] = through[k] + av * tile_of(spreads, S * k, j)
                    rated[k] = rated[k] + eg * r2
                    stepped = stepped + eg * dt
                    now[n, pl.ds(k, S, stride=K), :] = av * drive[h, k]
                part[n] += stepped
                sums = add_sums(sums, last, picker, n)
        g_write[jnp.minimum(h + 1, rows - 1)] = sums
        for k in range(K):
            g_feat[h, pl.ds(k, S, stride=K), :] = steps[h, k] * through[k]
            g_step[h, pl.ds(k, S, stride=K), :] = (
                column(feat, h, k, K) * through[k] + LN2 * rated[k])

    def states_pair(i):
        final_states(2 * i, even, odd)
        final_states(2 * i + 1, odd, even)

    def adjoint_pair(i):
        final_adjoint(rows - 1 - 2 * i, even, odd)
        final_adjoint(rows - 2 - 2 * i, odd, even)

    def last_sums():
        sums = jnp.zeros((NS, cols), F32)
        for n in range(NS):
            sums = add_sums(sums, odd, picker, n)
        return sums

    def send(src, dst, sems, kind, o, peer):
        copy = pltpu.make_async_remote_copy(
            src_ref=src, dst_ref=dst, send_sem=sems.at[kind, o], recv_sem=sems.at[kind + 1, o],
            device_id=peer, device_id_type=MESH)
        copy.start()
        return copy

    def arrive(copies):
        for copy in copies:
            copy.wait()

    mine_k, mine_h = pl.ds(ri * kr, kr), pl.ds(ci * hc, hc)

    def scatter_rows(source, box, kind):
        box[ri] = source(mine_k)[...]
        return [send(source(pl.ds(p[0] * kr, kr)), box.at[ri], row_sems, kind, o, p)
                for o, p in enumerate(row_peers)]

    def scatter_cols(source, box, kind):
        box[ci] = source(mine_h)[...]
        return [send(source(pl.ds(p[1] * hc, hc)), box.at[ci], col_sems, kind, o, p)
                for o, p in enumerate(col_peers)]

    def return_rows(box, target, kind):
        target(mine_k)[...] = box[ri]
        return [send(box.at[p[0]], target(mine_k), row_sems, kind, o, p)
                for o, p in enumerate(row_peers)]

    def return_cols(box, target, kind):
        target(mine_h)[...] = box[ci]
        return [send(box.at[p[1]], target(mine_h), col_sems, kind, o, p)
                for o, p in enumerate(col_peers)]

    def scan_cols(source, result, backward):
        for half in range(2):
            rate = slow[states_of(half), :]
            for j in range(hc):
                now = jnp.zeros((HALF, D), F32)
                for c in (reversed(range(nc)) if backward else range(nc)):
                    result[c, j, half] = now
                    now = jnp.exp2(rate * sums_c[c, j]) * now + source[c, j, half]

    lax.fori_loop(0, rows, code, 0, unroll=4)
    mid = rows // 2

    over(0, rows, functools.partial(local_vertical, 0))
    pl.semaphore_wait(barrier, len(row_peers) + len(col_peers))
    flights = [None, None]
    flights[0] = scatter_rows(lambda k: leave_v.at[0, k], in_v.at[0], 0)
    flights[0] += scatter_rows(lambda k: sum_rows.at[k], sums_r, 8)
    sum_flight = scatter_cols(lambda h: sum_cols.at[h], sums_c, 4)
    over(0, rows, functools.partial(local_vertical, 1))
    flights[1] = scatter_rows(lambda k: leave_v.at[1, k], in_v.at[1], 4)
    over(0, mid, local_adjoint)
    for half in range(2):
        arrive(flights[half])

        def scan_row(i, carry, half=half):
            r2 = rates[half * HALF + i]
            for j in range(kr):
                now = jnp.zeros((S, D), F32)
                for r in range(nr):
                    out_v[half, r, j, i] = now
                    now = jnp.exp2(r2 * sums_r[r, j]) * now + in_v[half, r, j, i]
            return carry

        lax.fori_loop(0, HALF, scan_row, 0)
        flights[half] = return_rows(out_v.at[half], lambda k: from_above.at[half, k], 2 + 4 * half)
    over(mid, rows, local_adjoint)
    right = scatter_cols(lambda h: leave_a.at[h], in_a, 0)
    arrive(flights[0])
    arrive(flights[1])
    vert[...] = from_above[...]
    over(0, mid, carried_states)
    arrive(sum_flight)
    arrive(right)
    scan_cols(in_a, out_a, True)
    right = return_cols(out_a, lambda h: from_right.at[h], 2)
    over(mid, rows, carried_states)
    left = scatter_cols(lambda h: leave_s.at[h], in_s, 6)
    arrive(right)
    over(0, mid, carried_adjoint)
    arrive(left)
    scan_cols(in_s, out_s, False)
    left = return_cols(out_s, lambda h: from_left.at[h], 8)
    over(mid, rows, carried_adjoint)
    under = scatter_rows(lambda k: leave_p.at[:, k], in_p, 10)
    arrive(left)
    over(0, mid // 2, states_pair)
    arrive(under)

    def scan_up(i, carry):
        for half in range(2):
            r2 = rates[half * HALF + i]
            for j in range(kr):
                now = jnp.zeros((S, D), F32)
                for r in reversed(range(nr)):
                    out_p[r, half, j, i] = now
                    now = jnp.exp2(r2 * sums_r[r, j]) * now + in_p[r, half, j, i]
        return carry

    lax.fori_loop(0, HALF, scan_up, 0)
    under = return_rows(out_p, lambda k: from_below.at[:, k], 12)
    over(mid // 2, mid, states_pair)
    g_read[rows - 1] = last_sums()
    arrive(under)
    over(0, mid, adjoint_pair)

    by_row[ri] = jnp.sum(part[...], axis=1)
    arrive([send(by_row.at[ri], by_row.at[ri], row_sems, 14, o, p)
            for o, p in enumerate(row_peers)])
    by_col[ci] = jnp.sum(by_row[...], axis=0)
    flight = [send(by_col.at[ci], by_col.at[ci], col_sems, 10, o, p)
              for o, p in enumerate(col_peers)]
    g_write[0] = last_sums()
    arrive(flight)
    g_decay[...] = jnp.sum(by_col[...], axis=0) * -jnp.exp(decay_log[...])


def shards(features, step_size, write_weights, read_weights, decay_log, out_grad):
    rows, cols = step_size.shape[0], step_size.shape[1]
    K = cols // S
    nr, nc = lax.axis_size("row"), lax.axis_size("col")
    kr, hc = K // nr, rows // nc

    def vm(*shape, kind=F32):
        return pltpu.VMEM(shape, kind)

    carry_r, carry_c = vm(2, K, HALF, S, D), vm(rows, 2, HALF, D)
    grid, kept = vm(rows, K, S, D), vm(rows, K, NS, S, D)
    joined = vm(rows, 2, S * HALF, D)
    box_v, box_p = vm(2, nr, kr, HALF, S, D), vm(nr, 2, kr, HALF, S, D)
    box_c = vm(nc, hc, 2, HALF, D)
    args = (features, step_size, write_weights.transpose(0, 2, 1),
            read_weights.transpose(0, 2, 1), out_grad, decay_log)
    outs = [(rows, cols, D), (rows, cols, D), (rows, NS, cols), (rows, NS, cols), (NS, D)]
    g_feat, g_step, g_write, g_read, g_decay = pl.pallas_call(
        functools.partial(scan_kernel, nr, nc),
        out_shape=[jax.ShapeDtypeStruct(o, F32) for o in outs],
        in_specs=[VMEM] * len(args),
        out_specs=[VMEM] * len(outs),
        scratch_shapes=[
            vm(NS, S, D), vm(NS, D), vm(3 * NS, NS * D, kind=BF16), vm(NS, NS, 2 * D, kind=BF16),
            vm(rows, 2 * cols, 3 * NS, kind=BF16), grid, grid, grid,
            vm(rows, S, D), vm(rows, S, D), vm(rows, 1, D), vm(K, S, D), joined, joined,
            vm(NS * S, D),
            carry_r, carry_r, carry_r, carry_r, carry_r,
            carry_c, carry_c, carry_c, carry_c, kept, kept,
            vm(NS, cols, D), vm(NS, cols, D), vm(NS, S, D),
            vm(nr, kr, S, D), vm(nc, hc, 1, D), box_v, box_v, box_p, box_p,
            box_c, box_c, box_c, box_c, vm(nr, NS, D), vm(nc, NS, D),
            pltpu.SemaphoreType.DMA((16, nr - 1)), pltpu.SemaphoreType.DMA((12, nc - 1))],
        compiler_params=pltpu.CompilerParams(
            collective_id=0, has_side_effects=True, vmem_limit_bytes=57 << 20),
        name="scan",
    )(*args)
    return (g_feat, g_step, g_write.transpose(0, 2, 1), g_read.transpose(0, 2, 1), g_decay)


def solution(mesh):
    tiles = P("row", "col", None)
    in_specs = (tiles, tiles, tiles, tiles, P(), tiles)
    out_specs = (tiles, tiles, tiles, tiles, P())
    return jax.shard_map(shards, mesh=mesh, in_specs=in_specs, out_specs=out_specs, check_vma=False)
```

time: 984 us -> 104 us (0.11); the launches traced: 968 us -> 104 us
  other arithmetic: 690 us -> 0 us
  Pallas kernels: 0 us -> 97.7 us
  local copies, waits for them, and re-layouts: 98.4 us -> 5.84 us
  matrix products: 74.7 us -> 0 us
  blocking collectives: 64.6 us -> 0 us
  waiting for transfers between devices: 23 us -> 0 us
  between operations: 14.6 us -> 0.65 us
    dynamic_update_slice x192 -> x0, other arithmetic: 376 us -> none  [the longest x64 143 us: sweep_rows(): closing, values = lax.scan(advance, initial, (decays, driving))]
    mul x100 -> x0, other arithmetic: 147 us -> none  [the longest x64 76.4 us: advance(): current = factor * value]
    pallas_call x0 -> x1, Pallas kernels: none -> 97.7 us  [shards(): pl.pallas_call(functools.partial(scan_kernel, nr, nc), out_shape=[jax.Sha...]
    select_n x48 -> x0, other arithmetic: 76.4 us -> none  [lap(): return jax.tree.map(lambda a, b: jnp.where(reached, a, b), new, before)]
    dot_general x3 -> x0, matrix products: 74.7 us -> none  [the longest x1 28.9 us: shards(): jnp.einsum('hwnd,hwd->hwn', adjoint_v, step_size * features, precision=hi...]
    psum x1 -> x0, blocking collectives: 64.6 us -> none  [shards(): grad_decay = lax.psum(partial_sum, ('row', 'col')) * decay_rate]
    add x2 -> x0, other arithmetic: 35.4 us -> none  [the longest x1 23.2 us: shards(): local_cols + jnp.exp(running_cols[:, :, None, :] * decay_rate) * from_lef...]
    dot_general x1 -> x0, other arithmetic: 34.8 us -> none  [shards(): jnp.einsum('hwnd,hwd->nd', exponent_grad, step_size, precision=highest)]
  transfers between devices with their start and end apart: 6 -> 0, of which waited for: 1 -> 0; matrix products, arithmetic and copies ran while one was open for 48% -> 0% of each run, Pallas kernels for 0% -> 0%
where the time goes in v4:
time: 104 us
  Pallas kernels  97.7 us (94%)
  local copies, waits for them, and re-layouts  5.84 us (6%)
    pallas_call x1, Pallas kernels, shards(): pl.pallas_call(functools.partial(scan_kernel, nr, nc), out_shape=[jax.Sha...  97.7 us
    unnamed x13, local copies, waits for them, and re-layouts  5.84 us

profile of v4, /device:TPU:1, one launch (start us, length us, event | category | flops | bytes accessed | tf_op | source)
XLA Modules:
  0.0 104.2 jit_solution(13152282578565203031)
XLA Ops:
  0.6 97.7 %scan.1 = (f32[32,64,128]{2,1,0:T(8,128)}, f32[32,64,128]{2,1,0:T(8,128)}, f32[32,16,64]{2,1,0:T(8,128)}, f32[32,16,64]{2,1,0:T(8,128)}, f32[16,128]{1,0:T(8,128)}) custom-call(f32[32,64,128]{2,1,0:T(8,128)} %feat.1, f32[32,64,128]{2,1,0:T(8,128)} %step.1, f32[32,16,64]{2,1,0:T(8,128)} %bitcast.4, f32[32,16,64]{2,1,0:T(8,128)} %bitcast.5, ...), custom_call_target="tpu_custom_call" | custom-call | tf_op jit(solution)/shard_map/scan/pallas_call | solution.py:437
  98.3 0.0 copy-start
  98.3 2.4 %copy.16 = f32[32,64,128]{2,1,0:T(8,128)} copy(f32[32,64,128]{2,1,0:T(8,128)} %get-tuple-element.20) | data formatting | bytes 2097152
  100.7 0.0 copy-done
  100.7 0.0 copy-start.2
  100.7 1.0 copy.17
  101.7 0.1 copy-done.2
  101.8 0.0 copy-start.1
  101.8 0.7 copy.18
  102.5 0.3 copy-done.1
  102.9 0.0 copy-start.3
  102.9 0.7 copy.19
  103.6 0.0 copy-done.3
  103.6 0.6 copy.20
Async XLA Ops:
  98.3 2.4 %copy-start = (f32[32,64,128]{2,1,0:T(8,128)S(1)}, f32[32,64,128]{2,1,0:T(8,128)}, u32[]{:S(2)}) copy-start(f32[32,64,128]{2,1,0:T(8,128)} %get-tuple-element.21) | copy-start | bytes 3145732
  100.7 1.1 %copy-start.2 = (f32[32,16,64]{2,1,0:T(8,128)S(1)}, f32[32,16,64]{2,1,0:T(8,128)}, u32[]{:S(2)}) copy-start(f32[32,16,64]{2,1,0:T(8,128)} %get-tuple-element.12) | copy-start | bytes 393220
  101.8 1.0 %copy-start.1 = (f32[32,16,64]{2,1,0:T(8,128)S(1)}, f32[32,16,64]{2,1,0:T(8,128)}, u32[]{:S(2)}) copy-start(f32[32,16,64]{2,1,0:T(8,128)} %get-tuple-element.13) | copy-start | bytes 393220
  102.9 0.7 copy-start.3

commit v5 on v4

v5 whole, which is shorter than its diff:
```python
import functools
import math
import jax
import jax.numpy as jnp
from jax import lax
from jax.experimental import pallas as pl
from jax.experimental.pallas import tpu as pltpu
from jax.sharding import PartitionSpec as P

NS = 16
HALF = 8
D = 128
S = 8
F32 = jnp.float32
BF16 = jnp.bfloat16
LOG2E = math.log2(math.e)
LN2 = math.log(2.0)
MESH = pl.DeviceIdType.MESH
VMEM = pl.BlockSpec(memory_space=pltpu.VMEM)


def column(ref, h, k, width):
    return ref[h, pl.ds(k, S, stride=width), :]


def set_rates(decay_log, rates):
    for n in range(NS):
        rates[n] = jnp.broadcast_to(-jnp.exp(decay_log[n : n + 1, :]) * LOG2E, (S, D))


def equal(a, b):
    return jnp.where(a == b, 1.0, 0.0).astype(BF16)


def set_spreaders(writes, reads, both):
    for table, parts in ((writes, (0,)), (reads, (1,)), (both, (0, 1))):
        row = lax.broadcasted_iota(jnp.int32, table.shape, 0)
        to = lax.broadcasted_iota(jnp.int32, table.shape, 1) // D
        if len(parts) == 1:
            meets = jnp.where(row // (3 * NS) == parts[0], row % NS, NS) == to
        else:
            meets = 2 * (row % NS) + row // (3 * NS) == to
        table[...] = jnp.where(meets, 1.0, 0.0).astype(BF16)


def by_segment(cols):
    K = cols // S
    at = lax.broadcasted_iota(jnp.int32, (cols, cols), 0)
    col = lax.broadcasted_iota(jnp.int32, (cols, cols), 1)
    return equal(col, (at % S) * K + at // S)


def split3(x, axis):
    high = x.astype(BF16)
    rest = x - high.astype(F32)
    mid = rest.astype(BF16)
    low = (rest - mid.astype(F32)).astype(BF16)
    return jnp.concatenate([high, mid, low], axis=axis)


def spread(coded, table, at):
    return jnp.dot(coded, table[:, 2 * D * at : 2 * D * at + 2 * D],
                   preferred_element_type=F32)


def sublane():
    return lax.broadcasted_iota(jnp.int32, (S, D), 0)


def sums_down(value, at):
    for shift in (1, 2, 4):
        value = value + jnp.where(at >= shift, pltpu.roll(value, shift, 0), 0.0)
    return value


def tile_of(block, row, half):
    return block[row : row + S, D * half : D * half + D]


def states_of(half):
    return slice(half * HALF, half * HALF + HALF)


def channel_sums(values, picker, n):
    high = values.astype(BF16)
    low = (values - high.astype(F32)).astype(BF16)
    return lax.dot_general(
        picker[n], jnp.concatenate([high, low], axis=1), (((1,), (1,)), ((), ())),
        preferred_element_type=F32)


def scan_kernel(nr, nc, feat, step, write, read, grad, decay_log,
                g_feat, g_step, g_write, g_read, g_decay,
                rates, slow, writes, reads, both, picker, coded, steps, grads, drive,
                before, upto, sum_cols, sum_rows, later, earlier, mix,
                leave_v, leave_p, vert, from_above, from_below,
                leave_a, leave_s, from_right, from_left, kept_s, kept_v, products, part,
                sums_r, sums_c, in_v, out_v, in_p, out_p, in_a, out_a, in_s, out_s,
                by_row, by_col, row_sems, col_sems):
    rows, cols = step.shape[0], step.shape[1]
    K = cols // S
    mid = rows // 2
    ri, ci = lax.axis_index("row"), lax.axis_index("col")
    kr, hc = K // nr, rows // nc
    row_peers = [(lax.rem(ri + o, nr), ci) for o in range(1, nr)]
    col_peers = [(ri, lax.rem(ci + o, nc)) for o in range(1, nc)]
    barrier = pltpu.get_barrier_semaphore()
    for peer in row_peers + col_peers:
        pl.semaphore_signal(barrier, inc=1, device_id=peer, device_id_type=MESH)

    set_rates(decay_log, rates)
    set_spreaders(writes, reads, both)
    slow[...] = -jnp.exp(decay_log[...]) * LOG2E
    picked = lax.broadcasted_iota(jnp.int32, picker.shape[1:], 0)
    for n in range(NS):
        picker[n] = equal(picked, n)
    leave_v[...] = jnp.zeros_like(leave_v)
    leave_p[...] = jnp.zeros_like(leave_p)
    sum_rows[...] = jnp.zeros_like(sum_rows)
    part[...] = jnp.zeros_like(part)
    at = sublane()
    turn = by_segment(cols)

    def code(h, carry):
        parts = jnp.concatenate([split3(write[h], 0), split3(read[h], 0)], axis=0)
        coded[pl.ds(pl.multiple_of(h * cols, cols), cols), :] = lax.dot_general(
            turn, parts, (((1,), (1,)), ((), ())), preferred_element_type=F32).astype(BF16)
        return carry

    def two_rows(i):
        return coded[pl.ds(pl.multiple_of(2 * cols * i, 2 * cols), 2 * cols), :]

    def each_state(codes, table, lo, hi):
        for pair in range(lo // 2, hi // 2):
            spreads = spread(codes, table, pair)
            for j in range(2):
                n = 2 * pair + j
                half, i = divmod(n, HALF)
                yield n, half, i, [
                    [tile_of(spreads, cols * u + S * k, j) for k in range(K)] for u in range(2)]

    def over(lo, hi, row):
        def one(i, carry):
            row(i)
            return carry

        lax.fori_loop(lo, hi, one, 0)

    def local_vertical(half, at_pair):
        pair = (2 * at_pair, 2 * at_pair + 1)
        if half == 0:
            for h in pair:
                total = jnp.zeros((S, D), F32)
                for k in range(K):
                    dt = column(step, h, k, K)
                    steps[h, k] = dt
                    drive[h, k] = dt * column(feat, h, k, K)
                    total = total + dt
                    sum_rows[k] += dt
                ends = sums_down(total, at)
                upto[h] = ends
                before[h] = ends - total
                sum_cols[h] = ends[S - 1 :, :]
        for n, _, i, wb in each_state(two_rows(at_pair), writes, half * HALF, half * HALF + HALF):
            r2 = rates[n]
            for k in range(K):
                v = leave_v[half, k, i]
                for u, h in enumerate(pair):
                    v = jnp.exp2(steps[h, k] * r2) * v + drive[h, k] * wb[u][k]
                leave_v[half, k, i] = v

    def local_adjoint(at_pair):
        pair = (2 * at_pair, 2 * at_pair + 1)
        for h in pair:
            for k in range(K):
                grads[h, k] = column(grad, h, k, K)
        for n, _, _, rb in each_state(two_rows(at_pair), reads, 0, NS):
            r2 = rates[n]
            for u, h in enumerate(pair):
                a = jnp.zeros((S, D), F32)
                for k in reversed(range(K)):
                    a = jnp.exp2(steps[h, k] * r2) * (a + rb[u][k] * grads[h, k])
                mix[u, S * n : S * n + S, :] = jnp.exp2(r2 * before[h]) * a
        for u, h in enumerate(pair):
            for half in range(2):
                passed = jnp.zeros((HALF, D), F32)
                for g in reversed(range(S)):
                    later[h, half, HALF * g : HALF * g + HALF, :] = passed
                    passed = passed + mix[u, pl.ds(S * HALF * half + g, HALF, stride=S), :]
                leave_a[h, half] = passed

    def carried_states(at_pair):
        pair = (2 * at_pair, 2 * at_pair + 1)
        for n, half, i, wb in each_state(two_rows(at_pair), writes, 0, NS):
            r2 = rates[n]
            l = [jnp.zeros((S, D), F32)] * 2
            for k in range(K):
                v = vert[half, k, i]
                for u, h in enumerate(pair):
                    e = jnp.exp2(steps[h, k] * r2)
                    v = e * v + drive[h, k] * wb[u][k]
                    l[u] = e * l[u] + v
                vert[half, k, i] = v
            for u, h in enumerate(pair):
                mix[u, S * n : S * n + S, :] = jnp.exp2(-r2 * upto[h]) * l[u]
        for u, h in enumerate(pair):
            for half in range(2):
                passed = jnp.zeros((HALF, D), F32)
                for g in range(S):
                    earlier[h, half, HALF * g : HALF * g + HALF, :] = passed
                    passed = passed + mix[u, pl.ds(S * HALF * half + g, HALF, stride=S), :]
                leave_s[h, half] = jnp.exp2(slow[states_of(half), :] * sum_cols[h]) * passed

    def enter(joined, h, half, entering):
        for g in range(S):
            at_g = slice(HALF * g, HALF * g + HALF)
            joined[h, half, at_g, :] = joined[h, half, at_g, :] + entering

    def carried_adjoint(i):
        at_pair = mid - 1 - i
        pair = (2 * at_pair, 2 * at_pair + 1)
        for h in pair:
            for half in range(2):
                enter(later, h, half,
                      jnp.exp2(slow[states_of(half), :] * sum_cols[h]) * from_right[h, half])
        for n, half, i, rb in each_state(two_rows(at_pair), reads, 0, NS):
            r2 = rates[n]
            a = [jnp.exp2(-r2 * upto[h]) * later[h, half, pl.ds(i, S, stride=HALF), :]
                 for h in pair]
            for k in reversed(range(K)):
                p = leave_p[half, k, i]
                for u in (1, 0):
                    h = pair[u]
                    e = jnp.exp2(steps[h, k] * r2)
                    ah = a[u] + rb[u][k] * grads[h, k]
                    p = e * (ah + p)
                    a[u] = e * ah
                leave_p[half, k, i] = p

    def store_sums(out, at_pair, sums):
        out[2 * at_pair] = sums[:, :cols]
        out[2 * at_pair + 1] = sums[:, cols:]

    def final_states(at_pair):
        pair = (2 * at_pair, 2 * at_pair + 1)
        for h in pair:
            for half in range(2):
                enter(earlier, h, half, from_left[h, half])
        sums = jnp.zeros((NS, 2 * cols), F32)
        for n, half, i, wb in each_state(two_rows(at_pair), writes, 0, NS):
            sums = sums + channel_sums(products[n], picker, n)
            r2 = rates[n]
            s = [jnp.exp2(r2 * before[h]) * earlier[h, half, pl.ds(i, S, stride=HALF), :]
                 for h in pair]
            for k in range(K):
                v = from_above[half, k, i]
                for u, h in enumerate(pair):
                    e = jnp.exp2(steps[h, k] * r2)
                    q = e * v
                    v = q + drive[h, k] * wb[u][k]
                    t = e * s[u]
                    s[u] = t + v
                    kept_v[h, k, n] = q
                    kept_s[h, k, n] = t
                    products[n, pl.ds(cols * u + k, S, stride=K), :] = s[u] * grads[h, k]
                from_above[half, k, i] = v
        store_sums(g_read, jnp.maximum(at_pair - 1, 0), sums)

    def final_adjoint(i):
        at_pair = mid - 1 - i
        pair = (2 * at_pair, 2 * at_pair + 1)
        codes = two_rows(at_pair)
        through = [[jnp.zeros((S, D), F32)] * K for _ in range(2)]
        rated = [[jnp.zeros((S, D), F32)] * K for _ in range(2)]
        sums = jnp.zeros((NS, 2 * cols), F32)
        for n in range(NS):
            half, i = divmod(n, HALF)
            spreads = spread(codes, both, n)
            sums = sums + channel_sums(products[n], picker, n)
            r2 = rates[n]
            a = [jnp.exp2(-r2 * upto[h]) * later[h, half, pl.ds(i, S, stride=HALF), :]
                 for h in pair]
            stepped = jnp.zeros((S, D), F32)
            for k in reversed(range(K)):
                b = from_below[half, k, i]
                for u in (1, 0):
                    h = pair[u]
                    dt = steps[h, k]
                    e = jnp.exp2(dt * r2)
                    ah = a[u] + tile_of(spreads, cols * u + S * k, 1) * grads[h, k]
                    av = ah + b
                    b = e * av
                    a[u] = e * ah
                    eg = ah * kept_s[h, k, n] + av * kept_v[h, k, n]
                    through[u][k] = through[u][k] + av * tile_of(spreads, cols * u + S * k, 0)
                    rated[u][k] = rated[u][k] + eg * r2
                    stepped = stepped + eg * dt
                    products[n, pl.ds(cols * u + k, S, stride=K), :] = av * drive[h, k]
                from_below[half, k, i] = b
            part[n] += stepped
        store_sums(g_write, jnp.minimum(at_pair + 1, mid - 1), sums)
        for u, h in enumerate(pair):
            for k in range(K):
                g_feat[h, pl.ds(k, S, stride=K), :] = steps[h, k] * through[u][k]
                g_step[h, pl.ds(k, S, stride=K), :] = (
                    column(feat, h, k, K) * through[u][k] + LN2 * rated[u][k])

    def last_sums():
        sums = jnp.zeros((NS, 2 * cols), F32)
        for n in range(NS):
            sums = sums + channel_sums(products[n], picker, n)
        return sums

    def send(src, dst, sems, kind, o, peer):
        copy = pltpu.make_async_remote_copy(
            src_ref=src, dst_ref=dst, send_sem=sems.at[kind, o], recv_sem=sems.at[kind + 1, o],
            device_id=peer, device_id_type=MESH)
        copy.start()
        return copy

    def arrive(copies):
        for copy in copies:
            copy.wait()

    mine_k, mine_h = pl.ds(ri * kr, kr), pl.ds(ci * hc, hc)

    def scatter_rows(source, box, kind):
        box[ri] = source(mine_k)[...]
        return [send(source(pl.ds(p[0] * kr, kr)), box.at[ri], row_sems, kind, o, p)
                for o, p in enumerate(row_peers)]

    def scatter_cols(source, box, kind):
        box[ci] = source(mine_h)[...]
        return [send(source(pl.ds(p[1] * hc, hc)), box.at[ci], col_sems, kind, o, p)
                for o, p in enumerate(col_peers)]

    def return_rows(box, target, kind):
        target(mine_k)[...] = box[ri]
        return [send(box.at[p[0]], target(mine_k), row_sems, kind, o, p)
                for o, p in enumerate(row_peers)]

    def return_cols(box, target, kind):
        target(mine_h)[...] = box[ci]
        return [send(box.at[p[1]], target(mine_h), col_sems, kind, o, p)
                for o, p in enumerate(col_peers)]

    def scan_cols(source, result, backward):
        for half in range(2):
            rate = slow[states_of(half), :]
            for j in range(hc):
                now = jnp.zeros((HALF, D), F32)
                for c in (reversed(range(nc)) if backward else range(nc)):
                    result[c, j, half] = now
                    now = jnp.exp2(rate * sums_c[c, j]) * now + source[c, j, half]

    lax.fori_loop(0, rows, code, 0, unroll=4)
    part_way = mid // 2

    over(0, mid, functools.partial(local_vertical, 0))
    pl.semaphore_wait(barrier, len(row_peers) + len(col_peers))
    flights = [None, None]
    flights[0] = scatter_rows(lambda k: leave_v.at[0, k], in_v.at[0], 0)
    flights[0] += scatter_rows(lambda k: sum_rows.at[k], sums_r, 8)
    sum_flight = scatter_cols(lambda h: sum_cols.at[h], sums_c, 4)
    over(0, mid, functools.partial(local_vertical, 1))
    flights[1] = scatter_rows(lambda k: leave_v.at[1, k], in_v.at[1], 4)
    over(0, part_way, local_adjoint)
    for half in range(2):
        arrive(flights[half])

        def scan_row(i, carry, half=half):
            r2 = rates[half * HALF + i]
            for j in range(kr):
                now = jnp.zeros((S, D), F32)
                for r in range(nr):
                    out_v[half, r, j, i] = now
                    now = jnp.exp2(r2 * sums_r[r, j]) * now + in_v[half, r, j, i]
            return carry

        lax.fori_loop(0, HALF, scan_row, 0)
        flights[half] = return_rows(out_v.at[half], lambda k: from_above.at[half, k], 2 + 4 * half)
    over(part_way, mid, local_adjoint)
    right = scatter_cols(lambda h: leave_a.at[h], in_a, 0)
    arrive(flights[0])
    arrive(flights[1])
    vert[...] = from_above[...]
    over(0, part_way, carried_states)
    arrive(sum_flight)
    arrive(right)
    scan_cols(in_a, out_a, True)
    right = return_cols(out_a, lambda h: from_right.at[h], 2)
    over(part_way, mid, carried_states)
    left = scatter_cols(lambda h: leave_s.at[h], in_s, 6)
    arrive(right)
    over(0, part_way, carried_adjoint)
    arrive(left)
    scan_cols(in_s, out_s, False)
    left = return_cols(out_s, lambda h: from_left.at[h], 8)
    over(part_way, mid, carried_adjoint)
    under = scatter_rows(lambda k: leave_p.at[:, k], in_p, 10)
    arrive(left)
    over(0, part_way, final_states)
    arrive(under)

    def scan_up(i, carry):
        for half in range(2):
            r2 = rates[half * HALF + i]
            for j in range(kr):
                now = jnp.zeros((S, D), F32)
                for r in reversed(range(nr)):
                    out_p[r, half, j, i] = now
                    now = jnp.exp2(r2 * sums_r[r, j]) * now + in_p[r, half, j, i]
        return carry

    lax.fori_loop(0, HALF, scan_up, 0)
    under = return_rows(out_p, lambda k: from_below.at[:, k], 12)
    over(part_way, mid, final_states)
    store_sums(g_read, mid - 1, last_sums())
    arrive(under)
    over(0, mid, final_adjoint)

    by_row[ri] = jnp.sum(part[...], axis=1)
    arrive([send(by_row.at[ri], by_row.at[ri], row_sems, 14, o, p)
            for o, p in enumerate(row_peers)])
    by_col[ci] = jnp.sum(by_row[...], axis=0)
    flight = [send(by_col.at[ci], by_col.at[ci], col_sems, 10, o, p)
              for o, p in enumerate(col_peers)]
    store_sums(g_write, 0, last_sums())
    arrive(flight)
    g_decay[...] = jnp.sum(by_col[...], axis=0) * -jnp.exp(decay_log[...])


def shards(features, step_size, write_weights, read_weights, decay_log, out_grad):
    rows, cols = step_size.shape[0], step_size.shape[1]
    K = cols // S
    nr, nc = lax.axis_size("row"), lax.axis_size("col")
    kr, hc = K // nr, rows // nc

    def vm(*shape, kind=F32):
        return pltpu.VMEM(shape, kind)

    carry_r, carry_c = vm(2, K, HALF, S, D), vm(rows, 2, HALF, D)
    grid, kept = vm(rows, K, S, D), vm(rows, K, NS, S, D)
    joined = vm(rows, 2, S * HALF, D)
    box_v, box_p = vm(2, nr, kr, HALF, S, D), vm(nr, 2, kr, HALF, S, D)
    table = vm(6 * NS, NS * D, kind=BF16)
    box_c = vm(nc, hc, 2, HALF, D)
    args = (features, step_size, write_weights.transpose(0, 2, 1),
            read_weights.transpose(0, 2, 1), out_grad, decay_log)
    outs = [(rows, cols, D), (rows, cols, D), (rows, NS, cols), (rows, NS, cols), (NS, D)]
    g_feat, g_step, g_write, g_read, g_decay = pl.pallas_call(
        functools.partial(scan_kernel, nr, nc),
        out_shape=[jax.ShapeDtypeStruct(o, F32) for o in outs],
        in_specs=[VMEM] * len(args),
        out_specs=[VMEM] * len(outs),
        scratch_shapes=[
            vm(NS, S, D), vm(NS, D), table, table, vm(6 * NS, 2 * NS * D, kind=BF16),
            vm(NS, NS, 2 * D, kind=BF16), vm(rows * cols, 6 * NS, kind=BF16), grid, grid, grid,
            vm(rows, S, D), vm(rows, S, D), vm(rows, 1, D), vm(K, S, D), joined, joined,
            vm(2, NS * S, D),
            carry_r, carry_r, carry_r, carry_r, carry_r,
            carry_c, carry_c, carry_c, carry_c, kept, kept,
            vm(NS, 2 * cols, D), vm(NS, S, D),
            vm(nr, kr, S, D), vm(nc, hc, 1, D), box_v, box_v, box_p, box_p,
            box_c, box_c, box_c, box_c, vm(nr, NS, D), vm(nc, NS, D),
            pltpu.SemaphoreType.DMA((16, nr - 1)), pltpu.SemaphoreType.DMA((12, nc - 1))],
        compiler_params=pltpu.CompilerParams(
            collective_id=0, has_side_effects=True, vmem_limit_bytes=57 << 20),
        name="scan",
    )(*args)
    return (g_feat, g_step, g_write.transpose(0, 2, 1), g_read.transpose(0, 2, 1), g_decay)


def solution(mesh):
    tiles = P("row", "col", None)
    in_specs = (tiles, tiles, tiles, tiles, P(), tiles)
    out_specs = (tiles, tiles, tiles, tiles, P())
    return jax.shard_map(shards, mesh=mesh, in_specs=in_specs, out_specs=out_specs, check_vma=False)
```

time: 104 us -> 101 us (0.971)
  Pallas kernels: 97.7 us -> 93.9 us
    pallas_call x1, Pallas kernels: 97.7 us -> 93.9 us  [shards(): pl.pallas_call(functools.partial(scan_kernel, nr, nc), out_shape=[jax.Sha...]
where the time goes in v5:
time: 101 us; the launch traced here: 100 us
  Pallas kernels  93.9 us (93%)
  local copies, waits for them, and re-layouts  5.84 us (6%)
    pallas_call x1, Pallas kernels, shards(): pl.pallas_call(functools.partial(scan_kernel, nr, nc), out_shape=[jax.Sha...  93.9 us
    unnamed x13, local copies, waits for them, and re-layouts  5.84 us

profile of v5, /device:TPU:1, one launch (start us, length us, event | category | flops | bytes accessed | tf_op | source)
XLA Modules:
  0.0 100.4 jit_solution(2509364816350327535)
XLA Ops:
  0.6 93.9 %scan.1 = (f32[32,64,128]{2,1,0:T(8,128)}, f32[32,64,128]{2,1,0:T(8,128)}, f32[32,16,64]{2,1,0:T(8,128)}, f32[32,16,64]{2,1,0:T(8,128)}, f32[16,128]{1,0:T(8,128)}) custom-call(f32[32,64,128]{2,1,0:T(8,128)} %feat.1, f32[32,64,128]{2,1,0:T(8,128)} %step.1, f32[32,16,64]{2,1,0:T(8,128)} %bitcast.4, f32[32,16,64]{2,1,0:T(8,128)} %bitcast.5, ...), custom_call_target="tpu_custom_call" | custom-call | tf_op jit(solution)/shard_map/scan/pallas_call | solution.py:451
  94.5 0.0 copy-start
  94.5 2.4 %copy.16 = f32[32,64,128]{2,1,0:T(8,128)} copy(f32[32,64,128]{2,1,0:T(8,128)} %get-tuple-element.20) | data formatting | bytes 2097152
  96.9 0.0 copy-done
  96.9 0.0 copy-start.2
  96.9 1.0 copy.17
  97.9 0.1 copy-done.2
  98.0 0.0 copy-start.1
  98.0 0.7 copy.18
  98.7 0.3 copy-done.1
  99.1 0.0 copy-start.3
  99.1 0.7 copy.19
  99.8 0.0 copy-done.3
  99.8 0.6 copy.20
Async XLA Ops:
  94.5 2.4 %copy-start = (f32[32,64,128]{2,1,0:T(8,128)S(1)}, f32[32,64,128]{2,1,0:T(8,128)}, u32[]{:S(2)}) copy-start(f32[32,64,128]{2,1,0:T(8,128)} %get-tuple-element.21) | copy-start | bytes 3145732
  96.9 1.1 %copy-start.2 = (f32[32,16,64]{2,1,0:T(8,128)S(1)}, f32[32,16,64]{2,1,0:T(8,128)}, u32[]{:S(2)}) copy-start(f32[32,16,64]{2,1,0:T(8,128)} %get-tuple-element.12) | copy-start | bytes 393220
  98.0 1.0 %copy-start.1 = (f32[32,16,64]{2,1,0:T(8,128)S(1)}, f32[32,16,64]{2,1,0:T(8,128)}, u32[]{:S(2)}) copy-start(f32[32,16,64]{2,1,0:T(8,128)} %get-tuple-element.13) | copy-start | bytes 393220
  99.1 0.7 copy-start.3

commit v6 on v5

--- a/solution.py
+++ b/solution.py
@@ -89,14 +89,14 @@
         preferred_element_type=F32)
 
 
-def scan_kernel(nr, nc, feat, step, write, read, grad, decay_log,
+def scan_kernel(nr, nc, feat, step, write, read, grad_far, decay_log,
                 g_feat, g_step, g_write, g_read, g_decay,
                 rates, slow, writes, reads, both, picker, coded, steps, grads, drive,
-                before, upto, sum_cols, sum_rows, later, earlier, mix,
-                leave_v, leave_p, vert, from_above, from_below,
+                before, upto, sum_cols, sum_rows, later, earlier,
+                leave_v, leave_p, from_above, from_below,
                 leave_a, leave_s, from_right, from_left, kept_s, kept_v, products, part,
-                sums_r, sums_c, in_v, out_v, in_p, out_p, in_a, out_a, in_s, out_s,
-                by_row, by_col, row_sems, col_sems):
+                sums_r, sums_c, in_r, out_r, in_c, out_c,
+                by_row, by_col, grad, row_sems, col_sems, grad_sem):
     rows, cols = step.shape[0], step.shape[1]
     K = cols // S
     mid = rows // 2
@@ -104,6 +104,8 @@
     kr, hc = K // nr, rows // nc
     row_peers = [(lax.rem(ri + o, nr), ci) for o in range(1, nr)]
     col_peers = [(ri, lax.rem(ci + o, nc)) for o in range(1, nc)]
+    fetch = pltpu.make_async_copy(grad_far, grad, grad_sem)
+    fetch.start()
     barrier = pltpu.get_barrier_semaphore()
     for peer in row_peers + col_peers:
         pl.semaphore_signal(barrier, inc=1, device_id=peer, device_id_type=MESH)
@@ -130,6 +132,11 @@
     def two_rows(i):
         return coded[pl.ds(pl.multiple_of(2 * cols * i, 2 * cols), 2 * cols), :]
 
+    def set_drive(pair):
+        for u, h in enumerate(pair):
+            for k in range(K):
+                drive[u, k] = steps[h, k] * column(feat, h, k, K)
+
     def each_state(codes, table, lo, hi):
         for pair in range(lo // 2, hi // 2):
             spreads = spread(codes, table, pair)
@@ -154,19 +161,19 @@
                 for k in range(K):
                     dt = column(step, h, k, K)
                     steps[h, k] = dt
-                    drive[h, k] = dt * column(feat, h, k, K)
                     total = total + dt
                     sum_rows[k] += dt
                 ends = sums_down(total, at)
                 upto[h] = ends
                 before[h] = ends - total
                 sum_cols[h] = ends[S - 1 :, :]
+        set_drive(pair)
         for n, _, i, wb in each_state(two_rows(at_pair), writes, half * HALF, half * HALF + HALF):
             r2 = rates[n]
             for k in range(K):
                 v = leave_v[half, k, i]
                 for u, h in enumerate(pair):
-                    v = jnp.exp2(steps[h, k] * r2) * v + drive[h, k] * wb[u][k]
+                    v = jnp.exp2(steps[h, k] * r2) * v + drive[u, k] * wb[u][k]
                 leave_v[half, k, i] = v
 
     def local_adjoint(at_pair):
@@ -180,50 +187,49 @@
                 a = jnp.zeros((S, D), F32)
                 for k in reversed(range(K)):
                     a = jnp.exp2(steps[h, k] * r2) * (a + rb[u][k] * grads[h, k])
-                mix[u, S * n : S * n + S, :] = jnp.exp2(r2 * before[h]) * a
+                products[u, S * n : S * n + S, :] = jnp.exp2(r2 * before[h]) * a
         for u, h in enumerate(pair):
             for half in range(2):
                 passed = jnp.zeros((HALF, D), F32)
                 for g in reversed(range(S)):
                     later[h, half, HALF * g : HALF * g + HALF, :] = passed
-                    passed = passed + mix[u, pl.ds(S * HALF * half + g, HALF, stride=S), :]
+                    passed = passed + products[u, pl.ds(S * HALF * half + g, HALF, stride=S), :]
                 leave_a[h, half] = passed
 
-    def carried_states(at_pair):
-        pair = (2 * at_pair, 2 * at_pair + 1)
-        for n, half, i, wb in each_state(two_rows(at_pair), writes, 0, NS):
+    def carried_states(half, at_pair):
+        pair = (2 * at_pair, 2 * at_pair + 1)
+        set_drive(pair)
+        for n, _, i, wb in each_state(two_rows(at_pair), writes, half * HALF, half * HALF + HALF):
             r2 = rates[n]
             l = [jnp.zeros((S, D), F32)] * 2
             for k in range(K):
-                v = vert[half, k, i]
+                v = leave_v[half, k, i]
                 for u, h in enumerate(pair):
                     e = jnp.exp2(steps[h, k] * r2)
-                    v = e * v + drive[h, k] * wb[u][k]
+                    v = e * v + drive[u, k] * wb[u][k]
                     l[u] = e * l[u] + v
-                vert[half, k, i] = v
+                leave_v[half, k, i] = v
             for u, h in enumerate(pair):
-                mix[u, S * n : S * n + S, :] = jnp.exp2(-r2 * upto[h]) * l[u]
+                products[u, S * n : S * n + S, :] = jnp.exp2(-r2 * upto[h]) * l[u]
         for u, h in enumerate(pair):
-            for half in range(2):
-                passed = jnp.zeros((HALF, D), F32)
-                for g in range(S):
-                    earlier[h, half, HALF * g : HALF * g + HALF, :] = passed
-                    passed = passed + mix[u, pl.ds(S * HALF * half + g, HALF, stride=S), :]
-                leave_s[h, half] = jnp.exp2(slow[states_of(half), :] * sum_cols[h]) * passed
+            passed = jnp.zeros((HALF, D), F32)
+            for g in range(S):
+                earlier[h, half, HALF * g : HALF * g + HALF, :] = passed
+                passed = passed + products[u, pl.ds(S * HALF * half + g, HALF, stride=S), :]
+            leave_s[h, half] = jnp.exp2(slow[states_of(half), :] * sum_cols[h]) * passed
 
     def enter(joined, h, half, entering):
         for g in range(S):
             at_g = slice(HALF * g, HALF * g + HALF)
             joined[h, half, at_g, :] = joined[h, half, at_g, :] + entering
 
-    def carried_adjoint(i):
+    def carried_adjoint(half, i):
         at_pair = mid - 1 - i
         pair = (2 * at_pair, 2 * at_pair + 1)
         for h in pair:
-            for half in range(2):
-                enter(later, h, half,
-                      jnp.exp2(slow[states_of(half), :] * sum_cols[h]) * from_right[h, half])
-        for n, half, i, rb in each_state(two_rows(at_pair), reads, 0, NS):
+            enter(later, h, half,
+                  jnp.exp2(slow[states_of(half), :] * sum_cols[h]) * from_right[h, half])
+        for n, _, i, rb in each_state(two_rows(at_pair), reads, half * HALF, half * HALF + HALF):
             r2 = rates[n]
             a = [jnp.exp2(-r2 * upto[h]) * later[h, half, pl.ds(i, S, stride=HALF), :]
                  for h in pair]
@@ -246,6 +252,7 @@
         for h in pair:
             for half in range(2):
                 enter(earlier, h, half, from_left[h, half])
+        set_drive(pair)
         sums = jnp.zeros((NS, 2 * cols), F32)
         for n, half, i, wb in each_state(two_rows(at_pair), writes, 0, NS):
             sums = sums + channel_sums(products[n], picker, n)
@@ -257,7 +264,7 @@
                 for u, h in enumerate(pair):
                     e = jnp.exp2(steps[h, k] * r2)
                     q = e * v
-                    v = q + drive[h, k] * wb[u][k]
+                    v = q + drive[u, k] * wb[u][k]
                     t = e * s[u]
                     s[u] = t + v
                     kept_v[h, k, n] = q
@@ -270,6 +277,7 @@
         at_pair = mid - 1 - i
         pair = (2 * at_pair, 2 * at_pair + 1)
         codes = two_rows(at_pair)
+        set_drive(pair)
         through = [[jnp.zeros((S, D), F32)] * K for _ in range(2)]
         rated = [[jnp.zeros((S, D), F32)] * K for _ in range(2)]
         sums = jnp.zeros((NS, 2 * cols), F32)
@@ -295,7 +303,7 @@
                     through[u][k] = through[u][k] + av * tile_of(spreads, cols * u + S * k, 0)
                     rated[u][k] = rated[u][k] + eg * r2
                     stepped = stepped + eg * dt
-                    products[n, pl.ds(cols * u + k, S, stride=K), :] = av * drive[h, k]
+                    products[n, pl.ds(cols * u + k, S, stride=K), :] = av * drive[u, k]
                 from_below[half, k, i] = b
             part[n] += stepped
         store_sums(g_write, jnp.minimum(at_pair + 1, mid - 1), sums)
@@ -325,8 +333,8 @@
     mine_k, mine_h = pl.ds(ri * kr, kr), pl.ds(ci * hc, hc)
 
     def scatter_rows(source, box, kind):
-        box[ri] = source(mine_k)[...]
-        return [send(source(pl.ds(p[0] * kr, kr)), box.at[ri], row_sems, kind, o, p)
+        box(ri)[...] = source(mine_k)[...]
+        return [send(source(pl.ds(p[0] * kr, kr)), box(ri), row_sems, kind, o, p)
                 for o, p in enumerate(row_peers)]
 
     def scatter_cols(source, box, kind):
@@ -335,8 +343,8 @@
                 for o, p in enumerate(col_peers)]
 
     def return_rows(box, target, kind):
-        target(mine_k)[...] = box[ri]
-        return [send(box.at[p[0]], target(mine_k), row_sems, kind, o, p)
+        target(mine_k)[...] = box(ri)[...]
+        return [send(box(p[0]), target(mine_k), row_sems, kind, o, p)
                 for o, p in enumerate(row_peers)]
 
     def return_cols(box, target, kind):
@@ -356,71 +364,72 @@
     lax.fori_loop(0, rows, code, 0, unroll=4)
     part_way = mid // 2
 
-    over(0, mid, functools.partial(local_vertical, 0))
-    pl.semaphore_wait(barrier, len(row_peers) + len(col_peers))
-    flights = [None, None]
-    flights[0] = scatter_rows(lambda k: leave_v.at[0, k], in_v.at[0], 0)
-    flights[0] += scatter_rows(lambda k: sum_rows.at[k], sums_r, 8)
-    sum_flight = scatter_cols(lambda h: sum_cols.at[h], sums_c, 4)
-    over(0, mid, functools.partial(local_vertical, 1))
-    flights[1] = scatter_rows(lambda k: leave_v.at[1, k], in_v.at[1], 4)
-    over(0, part_way, local_adjoint)
-    for half in range(2):
-        arrive(flights[half])
-
-        def scan_row(i, carry, half=half):
+    def scan_rows(half, backward):
+        def one(i, carry):
             r2 = rates[half * HALF + i]
             for j in range(kr):
                 now = jnp.zeros((S, D), F32)
-                for r in range(nr):
-                    out_v[half, r, j, i] = now
-                    now = jnp.exp2(r2 * sums_r[r, j]) * now + in_v[half, r, j, i]
+                for r in (reversed(range(nr)) if backward else range(nr)):
+                    out_r[r, half, j, i] = now
+                    now = jnp.exp2(r2 * sums_r[r, j]) * now + in_r[r, half, j, i]
             return carry
 
-        lax.fori_loop(0, HALF, scan_row, 0)
-        flights[half] = return_rows(out_v.at[half], lambda k: from_above.at[half, k], 2 + 4 * half)
+        lax.fori_loop(0, HALF, one, 0)
+
+    def rows_out(half, leave, kind):
+        return scatter_rows(lambda k: leave.at[half, k], lambda r: in_r.at[r, half], kind)
+
+    def rows_back(half, flight, backward, target, kind):
+        arrive(flight)
+        scan_rows(half, backward)
+        return return_rows(lambda r: out_r.at[r, half], lambda k: target.at[half, k], kind)
+
+    over(0, mid, functools.partial(local_vertical, 0))
+    pl.semaphore_wait(barrier, len(row_peers) + len(col_peers))
+    down = [None, None]
+    down[0] = rows_out(0, leave_v, 0)
+    down[0] += scatter_rows(lambda k: sum_rows.at[k], lambda r: sums_r.at[r], 8)
+    totals = scatter_cols(lambda h: sum_cols.at[h], sums_c, 4)
+    over(0, mid, functools.partial(local_vertical, 1))
+    down[1] = rows_out(1, leave_v, 4)
+    fetch.wait()
+    over(0, part_way, local_adjoint)
+    down[0] = rows_back(0, down[0], False, from_above, 2)
     over(part_way, mid, local_adjoint)
-    right = scatter_cols(lambda h: leave_a.at[h], in_a, 0)
-    arrive(flights[0])
-    arrive(flights[1])
-    vert[...] = from_above[...]
-    over(0, part_way, carried_states)
-    arrive(sum_flight)
+    right = scatter_cols(lambda h: leave_a.at[h], in_c, 0)
+    down[1] = rows_back(1, down[1], False, from_above, 6)
+    arrive(down[0])
+    leave_v[0] = from_above[0]
+    over(0, mid, functools.partial(carried_states, 0))
+    arrive(totals)
     arrive(right)
-    scan_cols(in_a, out_a, True)
-    right = return_cols(out_a, lambda h: from_right.at[h], 2)
-    over(part_way, mid, carried_states)
-    left = scatter_cols(lambda h: leave_s.at[h], in_s, 6)
+    scan_cols(in_c, out_c, True)
+    right = return_cols(out_c, lambda h: from_right.at[h], 2)
+    arrive(down[1])
+    leave_v[1] = from_above[1]
+    over(0, mid, functools.partial(carried_states, 1))
     arrive(right)
-    over(0, part_way, carried_adjoint)
+    left = scatter_cols(lambda h: leave_s.at[h], in_c, 6)
+    over(0, mid, functools.partial(carried_adjoint, 0))
+    up = [None, None]
+    up[0] = rows_out(0, leave_p, 10)
     arrive(left)
-    scan_cols(in_s, out_s, False)
-    left = return_cols(out_s, lambda h: from_left.at[h], 8)
-    over(part_way, mid, carried_adjoint)
-    under = scatter_rows(lambda k: leave_p.at[:, k], in_p, 10)
+    scan_cols(in_c, out_c, False)
+    left = return_cols(out_c, lambda h: from_left.at[h], 8)
+    over(0, mid, functools.partial(carried_adjoint, 1))
+    up[1] = rows_out(1, leave_p, 14)
     arrive(left)
     over(0, part_way, final_states)
-    arrive(under)
-
-    def scan_up(i, carry):
-        for half in range(2):
-            r2 = rates[half * HALF + i]
-            for j in range(kr):
-                now = jnp.zeros((S, D), F32)
-                for r in reversed(range(nr)):
-                    out_p[r, half, j, i] = now
-                    now = jnp.exp2(r2 * sums_r[r, j]) * now + in_p[r, half, j, i]
-        return carry
-
-    lax.fori_loop(0, HALF, scan_up, 0)
-    under = return_rows(out_p, lambda k: from_below.at[:, k], 12)
+    up[0] = rows_back(0, up[0], True, from_below, 12)
+    up[1] = rows_back(1, up[1], True, from_below, 16)
     over(part_way, mid, final_states)
     store_sums(g_read, mid - 1, last_sums())
-    arrive(under)
+    arrive(up[0])
+    arrive(up[1])
     over(0, mid, final_adjoint)
 
     by_row[ri] = jnp.sum(part[...], axis=1)
-    arrive([send(by_row.at[ri], by_row.at[ri], row_sems, 14, o, p)
+    arrive([send(by_row.at[ri], by_row.at[ri], row_sems, 18, o, p)
             for o, p in enumerate(row_peers)])
     by_col[ci] = jnp.sum(by_row[...], axis=0)
     flight = [send(by_col.at[ci], by_col.at[ci], col_sems, 10, o, p)
@@ -442,7 +451,7 @@
     carry_r, carry_c = vm(2, K, HALF, S, D), vm(rows, 2, HALF, D)
     grid, kept = vm(rows, K, S, D), vm(rows, K, NS, S, D)
     joined = vm(rows, 2, S * HALF, D)
-    box_v, box_p = vm(2, nr, kr, HALF, S, D), vm(nr, 2, kr, HALF, S, D)
+    box_r = vm(nr, 2, kr, HALF, S, D)
     table = vm(6 * NS, NS * D, kind=BF16)
     box_c = vm(nc, hc, 2, HALF, D)
     args = (features, step_size, write_weights.transpose(0, 2, 1),
@@ -451,21 +460,20 @@
     g_feat, g_step, g_write, g_read, g_decay = pl.pallas_call(
         functools.partial(scan_kernel, nr, nc),
         out_shape=[jax.ShapeDtypeStruct(o, F32) for o in outs],
-        in_specs=[VMEM] * len(args),
+        in_specs=[VMEM] * 4 + [pl.BlockSpec(memory_space=pl.ANY), VMEM],
         out_specs=[VMEM] * len(outs),
         scratch_shapes=[
             vm(NS, S, D), vm(NS, D), table, table, vm(6 * NS, 2 * NS * D, kind=BF16),
-            vm(NS, NS, 2 * D, kind=BF16), vm(rows * cols, 6 * NS, kind=BF16), grid, grid, grid,
+            vm(NS, NS, 2 * D, kind=BF16), vm(rows * cols, 6 * NS, kind=BF16), grid, grid, vm(2, K, S, D),
             vm(rows, S, D), vm(rows, S, D), vm(rows, 1, D), vm(K, S, D), joined, joined,
-            vm(2, NS * S, D),
-            carry_r, carry_r, carry_r, carry_r, carry_r,
+            carry_r, carry_r, carry_r, carry_r,
             carry_c, carry_c, carry_c, carry_c, kept, kept,
             vm(NS, 2 * cols, D), vm(NS, S, D),
-            vm(nr, kr, S, D), vm(nc, hc, 1, D), box_v, box_v, box_p, box_p,
-            box_c, box_c, box_c, box_c, vm(nr, NS, D), vm(nc, NS, D),
-            pltpu.SemaphoreType.DMA((16, nr - 1)), pltpu.SemaphoreType.DMA((12, nc - 1))],
+            vm(nr, kr, S, D), vm(nc, hc, 1, D), box_r, box_r, box_c, box_c, vm(nr, NS, D), vm(nc, NS, D), vm(rows, cols, D),
+            pltpu.SemaphoreType.DMA((20, nr - 1)), pltpu.SemaphoreType.DMA((12, nc - 1)),
+            pltpu.SemaphoreType.DMA],
         compiler_params=pltpu.CompilerParams(
-            collective_id=0, has_side_effects=True, vmem_limit_bytes=57 << 20),
+            collective_id=0, has_side_effects=True, vmem_limit_bytes=48 << 20),
         name="scan",
     )(*args)
     return (g_feat, g_step, g_write.transpose(0, 2, 1), g_read.transpose(0, 2, 1), g_decay)

time: 101 us -> 99.5 us (0.985)
  Pallas kernels: 93.9 us -> 89.6 us
  local copies, waits for them, and re-layouts: 5.84 us -> 8.98 us
    pallas_call x1, Pallas kernels: 93.9 us -> 89.6 us  [shards(): pl.pallas_call(functools.partial(scan_kernel, nr, nc), out_shape=[jax.Sha...]
    unnamed x13 -> x15, local copies, waits for them, and re-layouts: 5.84 us -> 8.98 us
where the time goes in v6:
time: 99.5 us; the launch traced here: 99.2 us
  Pallas kernels  89.6 us (90%)
  local copies, waits for them, and re-layouts  8.98 us (9%)
    pallas_call x1, Pallas kernels, shards(): pl.pallas_call(functools.partial(scan_kernel, nr, nc), out_shape=[jax.Sha...  89.6 us
    unnamed x15, local copies, waits for them, and re-layouts  8.98 us

profile of v6, /device:TPU:1, one launch (start us, length us, event | category | flops | bytes accessed | tf_op | source)
XLA Modules:
  0.0 99.2 jit_solution(7177864728144986134)
XLA Ops:
  0.6 0.0 copy-start
  0.6 1.2 %copy-done = f32[32,64,128]{2,1,0:T(8,128)S(1)} copy-done((f32[32,64,128]{2,1,0:T(8,128)S(1)}, f32[32,64,128]{2,1,0:T(8,128)}, u32[]{:S(2)}) %copy-start) | copy-done | bytes 1048600
  1.9 0.0 copy-start.1
  1.9 1.2 %copy-done.1 = f32[32,64,128]{2,1,0:T(8,128)S(1)} copy-done((f32[32,64,128]{2,1,0:T(8,128)S(1)}, f32[32,64,128]{2,1,0:T(8,128)}, u32[]{:S(2)}) %copy-start.1) | copy-done | bytes 1048600
  3.1 0.0 copy-start.2
  3.1 0.9 copy-done.2
  4.0 0.0 copy-start.3
  4.0 0.9 copy-done.3
  5.0 0.0 copy-start.4
  5.0 0.7 copy-done.4
  5.7 89.6 %scan.1 = (f32[32,64,128]{2,1,0:T(8,128)S(1)}, f32[32,64,128]{2,1,0:T(8,128)S(1)}, f32[32,16,64]{2,1,0:T(8,128)S(1)}, f32[32,16,64]{2,1,0:T(8,128)S(1)}, f32[16,128]{1,0:T(8,128)S(1)}) custom-call(f32[32,64,128]{2,1,0:T(8,128)S(1)} %copy-done, f32[32,64,128]{2,1,0:T(8,128)S(1)} %copy-done.1, f32[32,16,64]{2,1,0:T(8,128)S(1)} %bitcast.4, ...), custom_call_target="tpu_custom_call" | custom-call | tf_op jit(solution)/shard_map/scan/pallas_call | solution.py:460
  95.3 1.0 copy.16
  96.2 1.0 copy.17
  97.2 0.7 copy.18
  97.9 0.7 copy.19
  98.6 0.6 copy.20
Async XLA Ops:
  0.6 1.2 %copy-start = (f32[32,64,128]{2,1,0:T(8,128)S(1)}, f32[32,64,128]{2,1,0:T(8,128)}, u32[]{:S(2)}) copy-start(f32[32,64,128]{2,1,0:T(8,128)} %feat.1) | copy-start | bytes 3145732
  1.9 1.2 %copy-start.1 = (f32[32,64,128]{2,1,0:T(8,128)S(1)}, f32[32,64,128]{2,1,0:T(8,128)}, u32[]{:S(2)}) copy-start(f32[32,64,128]{2,1,0:T(8,128)} %step.1) | copy-start | bytes 3145732
  3.1 0.9 copy-start.2
  4.0 0.9 copy-start.3
  5.0 0.7 copy-start.4

commit v7 on v6

--- a/solution.py
+++ b/solution.py
@@ -89,23 +89,29 @@
         preferred_element_type=F32)
 
 
-def scan_kernel(nr, nc, feat, step, write, read, grad_far, decay_log,
+def scan_kernel(nr, nc, feat_far, step_far, write_far, read_far, grad_far, decay_log,
                 g_feat, g_step, g_write, g_read, g_decay,
                 rates, slow, writes, reads, both, picker, coded, steps, grads, drive,
-                before, upto, sum_cols, sum_rows, later, earlier,
+                before, upto, sum_cols, later, earlier,
                 leave_v, leave_p, from_above, from_below,
                 leave_a, leave_s, from_right, from_left, kept_s, kept_v, products, part,
-                sums_r, sums_c, in_r, out_r, in_c, out_c,
-                by_row, by_col, grad, row_sems, col_sems, grad_sem):
-    rows, cols = step.shape[0], step.shape[1]
+                in_r, out_r, in_c, out_c,
+                by_row, by_col, write, read, step, feat,
+                row_sems, col_sems, fetch_sems):
+    rows, cols = step_far.shape[0], step_far.shape[1]
     K = cols // S
     mid = rows // 2
     ri, ci = lax.axis_index("row"), lax.axis_index("col")
     kr, hc = K // nr, rows // nc
     row_peers = [(lax.rem(ri + o, nr), ci) for o in range(1, nr)]
     col_peers = [(ri, lax.rem(ci + o, nc)) for o in range(1, nc)]
-    fetch = pltpu.make_async_copy(grad_far, grad, grad_sem)
-    fetch.start()
+    fetches = [
+        pltpu.make_async_copy(far, near, fetch_sems.at[i])
+        for i, (far, near) in enumerate((
+            (write_far, write), (read_far, read), (step_far, step), (feat_far, feat),
+            (grad_far, products)))]
+    for fetch in fetches:
+        fetch.start()
     barrier = pltpu.get_barrier_semaphore()
     for peer in row_peers + col_peers:
         pl.semaphore_signal(barrier, inc=1, device_id=peer, device_id_type=MESH)
@@ -118,7 +124,6 @@
         picker[n] = equal(picked, n)
     leave_v[...] = jnp.zeros_like(leave_v)
     leave_p[...] = jnp.zeros_like(leave_p)
-    sum_rows[...] = jnp.zeros_like(sum_rows)
     part[...] = jnp.zeros_like(part)
     at = sublane()
     turn = by_segment(cols)
@@ -162,11 +167,12 @@
                     dt = column(step, h, k, K)
                     steps[h, k] = dt
                     total = total + dt
-                    sum_rows[k] += dt
+                    leave_v[0, k, HALF] += dt
                 ends = sums_down(total, at)
                 upto[h] = ends
                 before[h] = ends - total
                 sum_cols[h] = ends[S - 1 :, :]
+                leave_a[h, 2] = jnp.broadcast_to(ends[S - 1 :, :], (HALF, D))
         set_drive(pair)
         for n, _, i, wb in each_state(two_rows(at_pair), writes, half * HALF, half * HALF + HALF):
             r2 = rates[n]
@@ -176,11 +182,13 @@
                     v = jnp.exp2(steps[h, k] * r2) * v + drive[u, k] * wb[u][k]
                 leave_v[half, k, i] = v
 
+    def set_grads(at_pair):
+        for u in range(2):
+            for k in range(K):
+                grads[2 * at_pair + u, k] = products[at_pair, pl.ds(cols * u + k, S, stride=K), :]
+
     def local_adjoint(at_pair):
         pair = (2 * at_pair, 2 * at_pair + 1)
-        for h in pair:
-            for k in range(K):
-                grads[h, k] = column(grad, h, k, K)
         for n, _, _, rb in each_state(two_rows(at_pair), reads, 0, NS):
             r2 = rates[n]
             for u, h in enumerate(pair):
@@ -338,8 +346,8 @@
                 for o, p in enumerate(row_peers)]
 
     def scatter_cols(source, box, kind):
-        box[ci] = source(mine_h)[...]
-        return [send(source(pl.ds(p[1] * hc, hc)), box.at[ci], col_sems, kind, o, p)
+        box(ci)[...] = source(mine_h)[...]
+        return [send(source(pl.ds(p[1] * hc, hc)), box(ci), col_sems, kind, o, p)
                 for o, p in enumerate(col_peers)]
 
     def return_rows(box, target, kind):
@@ -359,9 +367,13 @@
                 now = jnp.zeros((HALF, D), F32)
                 for c in (reversed(range(nc)) if backward else range(nc)):
                     result[c, j, half] = now
-                    now = jnp.exp2(rate * sums_c[c, j]) * now + source[c, j, half]
-
+                    now = jnp.exp2(rate * source[c, j, 2]) * now + source[c, j, half]
+
+    fetches[0].wait()
+    fetches[1].wait()
     lax.fori_loop(0, rows, code, 0, unroll=4)
+    fetches[2].wait()
+    fetches[3].wait()
     part_way = mid // 2
 
     def scan_rows(half, backward):
@@ -371,13 +383,15 @@
                 now = jnp.zeros((S, D), F32)
                 for r in (reversed(range(nr)) if backward else range(nr)):
                     out_r[r, half, j, i] = now
-                    now = jnp.exp2(r2 * sums_r[r, j]) * now + in_r[r, half, j, i]
+                    now = jnp.exp2(r2 * in_r[r, 0, j, HALF]) * now + in_r[r, half, j, i]
             return carry
 
         lax.fori_loop(0, HALF, one, 0)
 
-    def rows_out(half, leave, kind):
-        return scatter_rows(lambda k: leave.at[half, k], lambda r: in_r.at[r, half], kind)
+    def rows_out(half, leave, kind, width=HALF):
+        part_of = pl.ds(0, width)
+        return scatter_rows(lambda k: leave.at[half, k, part_of],
+                            lambda r: in_r.at[r, half, :, part_of], kind)
 
     def rows_back(half, flight, backward, target, kind):
         arrive(flight)
@@ -387,29 +401,27 @@
     over(0, mid, functools.partial(local_vertical, 0))
     pl.semaphore_wait(barrier, len(row_peers) + len(col_peers))
     down = [None, None]
-    down[0] = rows_out(0, leave_v, 0)
-    down[0] += scatter_rows(lambda k: sum_rows.at[k], lambda r: sums_r.at[r], 8)
-    totals = scatter_cols(lambda h: sum_cols.at[h], sums_c, 4)
+    down[0] = rows_out(0, leave_v, 0, HALF + 1)
     over(0, mid, functools.partial(local_vertical, 1))
     down[1] = rows_out(1, leave_v, 4)
-    fetch.wait()
+    fetches[4].wait()
+    over(0, mid, set_grads)
     over(0, part_way, local_adjoint)
     down[0] = rows_back(0, down[0], False, from_above, 2)
     over(part_way, mid, local_adjoint)
-    right = scatter_cols(lambda h: leave_a.at[h], in_c, 0)
+    right = scatter_cols(lambda h: leave_a.at[h], lambda c: in_c.at[c], 0)
     down[1] = rows_back(1, down[1], False, from_above, 6)
     arrive(down[0])
-    leave_v[0] = from_above[0]
+    leave_v[0, :, :HALF] = from_above[0]
     over(0, mid, functools.partial(carried_states, 0))
-    arrive(totals)
     arrive(right)
     scan_cols(in_c, out_c, True)
     right = return_cols(out_c, lambda h: from_right.at[h], 2)
     arrive(down[1])
-    leave_v[1] = from_above[1]
+    leave_v[1, :, :HALF] = from_above[1]
     over(0, mid, functools.partial(carried_states, 1))
     arrive(right)
-    left = scatter_cols(lambda h: leave_s.at[h], in_c, 6)
+    left = scatter_cols(lambda h: leave_s.at[h], lambda c: in_c.at[c, :, pl.ds(0, 2)], 6)
     over(0, mid, functools.partial(carried_adjoint, 0))
     up = [None, None]
     up[0] = rows_out(0, leave_p, 10)
@@ -451,29 +463,31 @@
     carry_r, carry_c = vm(2, K, HALF, S, D), vm(rows, 2, HALF, D)
     grid, kept = vm(rows, K, S, D), vm(rows, K, NS, S, D)
     joined = vm(rows, 2, S * HALF, D)
+    raw = vm(rows, cols, D)
     box_r = vm(nr, 2, kr, HALF, S, D)
     table = vm(6 * NS, NS * D, kind=BF16)
     box_c = vm(nc, hc, 2, HALF, D)
     args = (features, step_size, write_weights.transpose(0, 2, 1),
-            read_weights.transpose(0, 2, 1), out_grad, decay_log)
+            read_weights.transpose(0, 2, 1), out_grad.reshape(NS, 2 * cols, D), decay_log)
     outs = [(rows, cols, D), (rows, cols, D), (rows, NS, cols), (rows, NS, cols), (NS, D)]
     g_feat, g_step, g_write, g_read, g_decay = pl.pallas_call(
         functools.partial(scan_kernel, nr, nc),
         out_shape=[jax.ShapeDtypeStruct(o, F32) for o in outs],
-        in_specs=[VMEM] * 4 + [pl.BlockSpec(memory_space=pl.ANY), VMEM],
+        in_specs=[pl.BlockSpec(memory_space=pl.ANY)] * 5 + [VMEM],
         out_specs=[VMEM] * len(outs),
         scratch_shapes=[
             vm(NS, S, D), vm(NS, D), table, table, vm(6 * NS, 2 * NS * D, kind=BF16),
             vm(NS, NS, 2 * D, kind=BF16), vm(rows * cols, 6 * NS, kind=BF16), grid, grid, vm(2, K, S, D),
-            vm(rows, S, D), vm(rows, S, D), vm(rows, 1, D), vm(K, S, D), joined, joined,
-            carry_r, carry_r, carry_r, carry_r,
-            carry_c, carry_c, carry_c, carry_c, kept, kept,
+            vm(rows, S, D), vm(rows, S, D), vm(rows, 1, D), joined, joined,
+            vm(2, K, HALF + 1, S, D), carry_r, carry_r, carry_r,
+            vm(rows, 3, HALF, D), carry_c, carry_c, carry_c, kept, kept,
             vm(NS, 2 * cols, D), vm(NS, S, D),
-            vm(nr, kr, S, D), vm(nc, hc, 1, D), box_r, box_r, box_c, box_c, vm(nr, NS, D), vm(nc, NS, D), vm(rows, cols, D),
+            vm(nr, 2, kr, HALF + 1, S, D), box_r, vm(nc, hc, 3, HALF, D), box_c, vm(nr, NS, D), vm(nc, NS, D),
+            vm(rows, NS, cols), vm(rows, NS, cols), raw, raw,
             pltpu.SemaphoreType.DMA((20, nr - 1)), pltpu.SemaphoreType.DMA((12, nc - 1)),
-            pltpu.SemaphoreType.DMA],
+            pltpu.SemaphoreType.DMA((5,))],
         compiler_params=pltpu.CompilerParams(
-            collective_id=0, has_side_effects=True, vmem_limit_bytes=48 << 20),
+            collective_id=0, has_side_effects=True, vmem_limit_bytes=50 << 20),
         name="scan",
     )(*args)
     return (g_feat, g_step, g_write.transpose(0, 2, 1), g_read.transpose(0, 2, 1), g_decay)

time: 99.5 us -> 97.6 us (0.981)
  local copies, waits for them, and re-layouts: 8.98 us -> 6.53 us
    unnamed x15 -> x11, local copies, waits for them, and re-layouts: 8.98 us -> 6.53 us
where the time goes in v7:
time: 97.6 us; the launch traced here: 97.4 us
  Pallas kernels  90.2 us (92%)
  local copies, waits for them, and re-layouts  6.53 us (7%)
    pallas_call x1, Pallas kernels, shards(): pl.pallas_call(functools.partial(scan_kernel, nr, nc), out_shape=[jax.Sha...  90.2 us
    unnamed x11, local copies, waits for them, and re-layouts  6.53 us

profile of v7, /device:TPU:1, one launch (start us, length us, event | category | flops | bytes accessed | tf_op | source)
XLA Modules:
  0.0 97.4 jit_solution(8416581127892528112)
XLA Ops:
  0.6 0.0 copy-start
  0.6 0.9 copy-done
  1.6 0.0 copy-start.1
  1.6 0.9 copy-done.1
  2.5 0.0 copy-start.2
  2.5 0.7 copy-done.2
  3.2 90.2 %scan.1 = (f32[32,64,128]{2,1,0:T(8,128)S(1)}, f32[32,64,128]{2,1,0:T(8,128)S(1)}, f32[32,16,64]{2,1,0:T(8,128)S(1)}, f32[32,16,64]{2,1,0:T(8,128)S(1)}, f32[16,128]{1,0:T(8,128)S(1)}) custom-call(f32[32,64,128]{2,1,0:T(8,128)} %feat_far.1, f32[32,64,128]{2,1,0:T(8,128)} %step_far.1, f32[32,16,64]{2,1,0:T(8,128)S(1)} %bitcast.5, f32[32,16,64]{2,1,0:T(8,128)S(1)} %bitcast.6, ...), custom_call_target="tpu_custom_call" | custom-call | tf_op jit(solution)/shard_map/scan/pallas_call | solution.py:473
  93.4 1.0 copy.16
  94.4 1.0 copy.17
  95.4 0.7 copy.18
  96.1 0.7 copy.19
  96.8 0.6 copy.20
Async XLA Ops:
  0.6 1.0 copy-start
  1.6 0.9 copy-start.1
  2.5 0.7 copy-start.2

commit v8 on v7

--- a/solution.py
+++ b/solution.py
@@ -431,8 +431,9 @@
     over(0, mid, functools.partial(carried_adjoint, 1))
     up[1] = rows_out(1, leave_p, 14)
     arrive(left)
-    over(0, part_way, final_states)
+    over(0, part_way // 2, final_states)
     up[0] = rows_back(0, up[0], True, from_below, 12)
+    over(part_way // 2, part_way, final_states)
     up[1] = rows_back(1, up[1], True, from_below, 16)
     over(part_way, mid, final_states)
     store_sums(g_read, mid - 1, last_sums())

time: 97.6 us -> 97.5 us (level)
  no operation moved by 1% of the time
where the time goes in v8:
time: 97.5 us; the launch traced here: 97.3 us
  Pallas kernels  90.1 us (92%)
  local copies, waits for them, and re-layouts  6.53 us (7%)
    pallas_call x1, Pallas kernels, shards(): pl.pallas_call(functools.partial(scan_kernel, nr, nc), out_shape=[jax.Sha...  90.1 us
    unnamed x11, local copies, waits for them, and re-layouts  6.53 us

profile of v8, /device:TPU:1, one launch (start us, length us, event | category | flops | bytes accessed | tf_op | source)
XLA Modules:
  0.0 97.3 jit_solution(12731630164430273841)
XLA Ops:
  0.6 0.0 copy-start
  0.6 0.9 copy-done
  1.6 0.0 copy-start.1
  1.6 0.9 copy-done.1
  2.5 0.0 copy-start.2
  2.5 0.7 copy-done.2
  3.2 90.1 %scan.1 = (f32[32,64,128]{2,1,0:T(8,128)S(1)}, f32[32,64,128]{2,1,0:T(8,128)S(1)}, f32[32,16,64]{2,1,0:T(8,128)S(1)}, f32[32,16,64]{2,1,0:T(8,128)S(1)}, f32[16,128]{1,0:T(8,128)S(1)}) custom-call(f32[32,64,128]{2,1,0:T(8,128)} %feat_far.1, f32[32,64,128]{2,1,0:T(8,128)} %step_far.1, f32[32,16,64]{2,1,0:T(8,128)S(1)} %bitcast.5, f32[32,16,64]{2,1,0:T(8,128)S(1)} %bitcast.6, ...), custom_call_target="tpu_custom_call" | custom-call | tf_op jit(solution)/shard_map/scan/pallas_call | solution.py:474
  93.3 1.0 copy.16
  94.3 1.0 copy.17
  95.3 0.7 copy.18
  96.0 0.7 copy.19
  96.7 0.6 copy.20
Async XLA Ops:
  0.6 1.0 copy-start
  1.6 0.9 copy-start.1
  2.5 0.7 copy-start.2
